TPU v7x, 128 devices: a whole 4x4x4 slice. The times are simulated.
128 devices in a mesh: tile: 16 (over y, z_lo, core), frame: 8 (over z_hi, x).
Axes of the slice: x: 4, y: 4, z: 4 (z_hi: 2, z_lo: 2; z = z_hi * 2 + z_lo), core: 2. Of those that a mesh axis runs over, the one named last changes fastest.
Arguments:
- object_slices: float32 [2, 2, 4096, 1024], P(None, None, 'tile', 'frame'), may hold values from -6 to 6
- probe_modes: float32 [2, 2, 256, 256], replicated, may hold values from -3 to 3
- prop_phase: float32 [256, 256], replicated, may hold values from -3.140625 to 3.140625
- background: float32 [256, 256], replicated, may hold values from 0.1 to 1
- positions: int32 [256, 2], P(('tile', 'frame')), may hold values from 0 to 768, as said below
- counts: int32 [256, 256, 256], P(('tile', 'frame')), may hold values from 0 to 8
Outputs:
- object_grad: float32 [2, 2, 4096, 1024], P(None, None, 'tile', 'frame')
- probe_grad: float32 [2, 2, 256, 256], replicated
Inputs may be any that keep to these rules, and one draw needn't show every extreme that they name: `positions`: rows lie in 0 to 256, columns in 0 to 768.
All inputs are finite; a program needn't handle non-finite values.
Results may differ from a plain program's by a relative error of at most 0.0003.
Values sent between devices are 32-bit elements; how exact they have to be, the bound alone decides.
A program may use at most 128 MiB of HBM per device.

v0:
```python
import functools
import numpy as np
import ml_dtypes
import jax
import jax.numpy as jnp
from jax import lax
from jax.experimental import pallas as pl
from jax.experimental.pallas import tpu as pltpu
from jax.sharding import PartitionSpec as P

FRAME = 256
HALF = 128
SLICES = 2
MODES = 2
HALO = 128
ROWS_EXT = 512
STRIPS = 8
WIN_ROWS = 264
WIN_COLS = 384
CHUNK = 32
F32 = jnp.float32
BF16 = jnp.bfloat16


def dft_constants():
    k = np.arange(HALF)[:, None]
    n = np.arange(HALF)[None, :]
    mats = []
    for odd in (0, 1):
        turns = ((2 * k + odd) * n) % FRAME
        angle = -2.0 * np.pi * turns / FRAME
        c, s = np.cos(angle) / 16.0, np.sin(angle) / 16.0
        mats.append(np.block([[c, -s], [s, c]]))
    even, odd = mats
    lefts, rights = [], []
    for m in (even, odd, even.T, odd.T):
        hi = m.astype(ml_dtypes.bfloat16)
        lo = (m - hi.astype(np.float64)).astype(ml_dtypes.bfloat16)
        lefts.append(np.concatenate([hi, hi, lo], axis=1))
        rights.append(np.concatenate([hi, hi, lo], axis=0))
    perm = np.zeros((FRAME, FRAME))
    order = np.concatenate([np.arange(0, FRAME, 2), np.arange(1, FRAME, 2)])
    perm[np.arange(FRAME), order] = 1.0
    perms = np.stack([perm, perm.T]).astype(ml_dtypes.bfloat16)
    return np.stack(lefts), np.stack(rights), perms


def mm(a, b):
    return jnp.dot(a, b, preferred_element_type=F32)


def parts3(x):
    a = x.astype(BF16)
    r = x - a.astype(F32)
    b = r.astype(BF16)
    c = (r - b.astype(F32)).astype(BF16)
    return a, b, c


def reorder_exact(x, perm, perm_t):
    a, b, c = parts3(x)
    y = mm(perm, a) + mm(perm, b) + mm(perm, c)
    a, b, c = parts3(y)
    return mm(a, perm_t) + mm(b, perm_t) + mm(c, perm_t)


def frame_kernel(
    pos_ref, ext_ref, probe_ref, phase_ref, back_ref, counts_ref, left_ref, right_ref, perm_ref,
    grad_ref, probe_out_ref,
    win, obj, kern, bg, cnt, wave, u1, rop, lop, tmp, freq, win_sems,
):
    def corner(f):
        r = pos_ref[f, 0]
        c = pos_ref[f, 1]
        r8 = jnp.minimum(r // 8, 31) * 8
        cs = jnp.minimum(c // HALF, 5)
        return r, c, pl.multiple_of(r8, 8), cs

    def window_copies(f):
        _, _, r8, cs = corner(f)
        return [
            pltpu.make_async_copy(
                ext_ref.at[cs + j, :, :, pl.ds(r8, WIN_ROWS), :],
                win.at[f, :, :, :, pl.ds(j * HALF, HALF)],
                win_sems.at[f, j],
            )
            for j in range(3)
        ]

    for f in range(2):
        for copy in window_copies(f):
            copy.start()

    perm, perm_t = perm_ref[0], perm_ref[1]
    bg[...] = reorder_exact(back_ref[...], perm, perm_t)
    phase = reorder_exact(phase_ref[...], perm, perm_t)
    kern[0] = jnp.cos(phase)
    kern[1] = jnp.sin(phase)
    for f in range(2):
        half = mm(perm, counts_ref[f].astype(F32).astype(BF16)).astype(BF16)
        cnt[f] = mm(half, perm_t)

    grad_ref[...] = jnp.zeros_like(grad_ref)

    def put_right(m, parity, rows, x):
        hi = x.astype(BF16)
        lo = (x - hi.astype(F32)).astype(BF16)
        rop[m, parity, rows, 0:256] = hi
        rop[m, parity, rows, 256:512] = lo
        rop[m, parity, rows, 512:768] = hi

    def put_left(m, parity, start, x):
        hi = x.astype(BF16)
        lo = (x - hi.astype(F32)).astype(BF16)
        n = x.shape[0]
        lop[m, parity, pl.ds(start, n), :] = hi
        lop[m, parity, pl.ds(256 + start, n), :] = lo
        lop[m, parity, pl.ds(512 + start, n), :] = hi

    def forward(m, produce):
        for q in range(FRAME // CHUNK):
            rows = pl.ds(q * CHUNK, CHUNK)
            re, im = produce(m, rows)
            a, b = re[:, :HALF], re[:, HALF:]
            c, d = im[:, :HALF], im[:, HALF:]
            put_right(m, 0, rows, jnp.concatenate([a + b, c + d], axis=1))
            put_right(m, 1, rows, jnp.concatenate([a - b, c - d], axis=1))
        tmp[m, 0] = mm(rop[m, 0], right_ref[2])
        tmp[m, 1] = mm(rop[m, 1], right_ref[3])
        for q in range(HALF // CHUNK):
            top = pl.ds(q * CHUNK, CHUNK)
            bot = pl.ds(HALF + q * CHUNK, CHUNK)
            et, eb = tmp[m, 0, top, :], tmp[m, 0, bot, :]
            ot, ob = tmp[m, 1, top, :], tmp[m, 1, bot, :]
            for parity, e, o in ((0, et + eb, ot + ob), (1, et - eb, ot - ob)):
                put_left(m, parity, q * CHUNK, jnp.concatenate([e[:, :HALF], o[:, :HALF]], axis=1))
                put_left(m, parity, HALF + q * CHUNK, jnp.concatenate([e[:, HALF:], o[:, HALF:]], axis=1))
        freq[m, 0] = mm(left_ref[0], lop[m, 0])
        freq[m, 1] = mm(left_ref[1], lop[m, 1])

    def backward(m, modify, consume):
        for parity in range(2):
            for q in range(HALF // CHUNK):
                top = pl.ds(q * CHUNK, CHUNK)
                bot = pl.ds(HALF + q * CHUNK, CHUNK)
                table_rows = pl.ds(parity * HALF + q * CHUNK, CHUNK)
                re, im = modify(table_rows, freq[m, parity, top, :], freq[m, parity, bot, :])
                put_left(m, parity, q * CHUNK, re)
                put_left(m, parity, HALF + q * CHUNK, im)
        tmp[m, 0] = mm(left_ref[2], lop[m, 0])
        tmp[m, 1] = mm(left_ref[3], lop[m, 1])
        for q in range(HALF // CHUNK):
            top = pl.ds(q * CHUNK, CHUNK)
            bot = pl.ds(HALF + q * CHUNK, CHUNK)
            gr, gi = tmp[m, 0, top, :], tmp[m, 0, bot, :]
            hr, hi = tmp[m, 1, top, :], tmp[m, 1, bot, :]
            for rows, re, im in ((top, gr + hr, gi + hi), (bot, gr - hr, gi - hi)):
                put_right(m, 0, rows, jnp.concatenate([re[:, :HALF], im[:, :HALF]], axis=1))
                put_right(m, 1, rows, jnp.concatenate([re[:, HALF:], im[:, HALF:]], axis=1))
        tmp[m, 0] = mm(rop[m, 0], right_ref[0])
        tmp[m, 1] = mm(rop[m, 1], right_ref[1])
        for q in range(FRAME // CHUNK):
            rows = pl.ds(q * CHUNK, CHUNK)
            g, h = tmp[m, 0, rows, :], tmp[m, 1, rows, :]
            re = jnp.concatenate([g[:, :HALF] + h[:, :HALF], g[:, :HALF] - h[:, :HALF]], axis=1)
            im = jnp.concatenate([g[:, HALF:] + h[:, HALF:], g[:, HALF:] - h[:, HALF:]], axis=1)
            consume(m, rows, re, im)

    @pl.loop(0, 2)
    def _(f):
        r, c, r8, cs = corner(f)
        row_shift = r - r8
        col_shift = c - cs * HALF
        for copy in window_copies(f):
            copy.wait()

        for s in range(SLICES):
            for p in range(2):
                for q in range(FRAME // CHUNK):
                    x = win[f, s, p, pl.ds(q * CHUNK, CHUNK + 8), :]
                    x = pltpu.roll(x, lax.rem(WIN_COLS - col_shift, WIN_COLS), 1)[:, :FRAME]
                    x = pltpu.roll(x, lax.rem(CHUNK + 8 - row_shift, CHUNK + 8), 0)
                    obj[s, p, pl.ds(q * CHUNK, CHUNK), :] = x[:CHUNK]

        def enter(m, rows):
            pr, pi = probe_ref[m, 0, rows, :], probe_ref[m, 1, rows, :]
            a, b = obj[0, 0, rows, :], obj[0, 1, rows, :]
            return pr * a - pi * b, pr * b + pi * a

        def through(m, rows):
            ur, ui = u1[m, 0, rows, :], u1[m, 1, rows, :]
            a, b = obj[1, 0, rows, :], obj[1, 1, rows, :]
            return ur * a - ui * b, ur * b + ui * a

        def returning(m, rows):
            hr, hi = wave[m, 0, rows, :], wave[m, 1, rows, :]
            a, b = obj[1, 0, rows, :], obj[1, 1, rows, :]
            return hr * a + hi * b, hi * a - hr * b

        def propagator(rows, re, im):
            kr, ki = kern[0, rows, :], kern[1, rows, :]
            return re * kr - im * ki, re * ki + im * kr

        def adjoint(rows, re, im):
            kr, ki = kern[0, rows, :], kern[1, rows, :]
            return re * kr + im * ki, im * kr - re * ki

        def weighted(rows, re, im):
            w = cnt[f, rows, :]
            return re * w, im * w

        def keep_u1(m, rows, re, im):
            u1[m, 0, rows, :] = re
            u1[m, 1, rows, :] = im

        def keep_wave(m, rows, re, im):
            wave[m, 0, rows, :] = re
            wave[m, 1, rows, :] = im

        def scatter(s, source):
            for q in range(FRAME // CHUNK):
                rows = pl.ds(q * CHUNK, CHUNK)
                target = pl.ds(pl.multiple_of(r8 + q * CHUNK, 8), CHUNK + 8)
                gr = gi = None
                for m in range(MODES):
                    ur, ui = source(m, rows)
                    hr, hi = wave[m, 0, rows, :], wave[m, 1, rows, :]
                    tr, ti = ur * hr + ui * hi, ur * hi - ui * hr
                    gr, gi = (tr, ti) if gr is None else (gr + tr, gi + ti)
                below = jnp.zeros((8, FRAME), F32)
                beside = jnp.zeros((CHUNK + 8, HALF), F32)
                for p, g in enumerate((gr, gi)):
                    tall = pltpu.roll(jnp.concatenate([g, below], axis=0), row_shift, 0)
                    wide = pltpu.roll(jnp.concatenate([tall, beside], axis=1), col_shift, 1)
                    for j in range(3):
                        grad_ref[cs + j, s, p, target, :] += wide[:, j * HALF:(j + 1) * HALF]

        for m in range(MODES):
            forward(m, enter)
        for m in range(MODES):
            backward(m, propagator, keep_u1)
        for m in range(MODES):
            forward(m, through)
        for parity in range(2):
            for q in range(HALF // CHUNK):
                top = pl.ds(q * CHUNK, CHUNK)
                bot = pl.ds(HALF + q * CHUNK, CHUNK)
                rows = pl.ds(parity * HALF + q * CHUNK, CHUNK)
                level = bg[rows, :]
                for m in range(MODES):
                    re, im = freq[m, parity, top, :], freq[m, parity, bot, :]
                    level = level + re * re + im * im
                cnt[f, rows, :] = 1.0 - cnt[f, rows, :] / level
        for m in range(MODES):
            backward(m, weighted, keep_wave)
        scatter(1, lambda m, rows: (u1[m, 0, rows, :], u1[m, 1, rows, :]))
        for m in range(MODES):
            forward(m, returning)
        for m in range(MODES):
            backward(m, adjoint, keep_wave)
        scatter(0, lambda m, rows: (probe_ref[m, 0, rows, :], probe_ref[m, 1, rows, :]))
        for m in range(MODES):
            for q in range(FRAME // CHUNK):
                rows = pl.ds(q * CHUNK, CHUNK)
                hr, hi = wave[m, 0, rows, :], wave[m, 1, rows, :]
                a, b = obj[0, 0, rows, :], obj[0, 1, rows, :]
                tr, ti = hr * a + hi * b, hi * a - hr * b

                @pl.when(f == 0)
                def _():
                    probe_out_ref[m, 0, rows, :] = tr
                    probe_out_ref[m, 1, rows, :] = ti

                @pl.when(f != 0)
                def _():
                    probe_out_ref[m, 0, rows, :] += tr
                    probe_out_ref[m, 1, rows, :] += ti


def frame_terms(positions, ext, probe_modes, prop_phase, background, counts):
    lefts, rights, perms = dft_constants()
    vmem = pl.BlockSpec(memory_space=pltpu.VMEM)
    square = (FRAME, FRAME)
    return pl.pallas_call(
        frame_kernel,
        out_shape=(
            jax.ShapeDtypeStruct((STRIPS, SLICES, 2, ROWS_EXT, HALF), F32),
            jax.ShapeDtypeStruct((MODES, 2) + square, F32),
        ),
        in_specs=[pl.BlockSpec(memory_space=pltpu.SMEM), pl.BlockSpec(memory_space=pl.ANY)] + [vmem] * 7,
        out_specs=(vmem, vmem),
        scratch_shapes=[
            pltpu.VMEM((2, SLICES, 2, WIN_ROWS, WIN_COLS), F32),
            pltpu.VMEM((SLICES, 2) + square, F32),
            pltpu.VMEM((2,) + square, F32),
            pltpu.VMEM(square, F32),
            pltpu.VMEM((2,) + square, F32),
            pltpu.VMEM((MODES, 2) + square, F32),
            pltpu.VMEM((MODES, 2) + square, F32),
            pltpu.VMEM((MODES, 2, FRAME, 3 * FRAME), BF16),
            pltpu.VMEM((MODES, 2, 3 * FRAME, FRAME), BF16),
            pltpu.VMEM((MODES, 2) + square, F32),
            pltpu.VMEM((MODES, 2) + square, F32),
            pltpu.SemaphoreType.DMA((2, 3)),
        ],
        compiler_params=pltpu.CompilerParams(vmem_limit_bytes=48 << 20),
        name="frame_terms",
    )(positions, ext, probe_modes, prop_phase, background, counts,
      jnp.asarray(lefts), jnp.asarray(rights), jnp.asarray(perms))


def shifted(array, axis, by):
    count = lax.axis_size(axis)
    return lax.ppermute(array, axis, [(i, (i + by) % count) for i in range(count)])


def shards(object_slices, probe_modes, prop_phase, background, positions, counts):
    rows_own = object_slices.shape[2]
    before = shifted(object_slices[:, :, rows_own - HALO:], "tile", 1)
    after = shifted(object_slices[:, :, :HALO], "tile", -1)
    strip = jnp.concatenate([before, object_slices, after], axis=2)
    ext = lax.all_gather(strip, "frame", axis=0, tiled=False)
    grads, probe_term = frame_terms(positions, ext, probe_modes, prop_phase, background, counts)
    probe_grad = lax.psum(probe_term, ("tile", "frame"))
    summed = lax.psum_scatter(grads, "frame", scatter_dimension=0, tiled=False)
    from_below = shifted(summed[:, :, :HALO], "tile", -1)
    from_above = shifted(summed[:, :, HALO + rows_own:], "tile", 1)
    object_grad = summed[:, :, HALO:HALO + rows_own]
    object_grad = object_grad.at[:, :, rows_own - HALO:].add(from_below)
    object_grad = object_grad.at[:, :, :HALO].add(from_above)
    return object_grad, probe_grad


def solution(mesh):
    in_specs = (
        P(None, None, "tile", "frame"),
        P(),
        P(),
        P(),
        P(("tile", "frame"), None),
        P(("tile", "frame"), None, None),
    )
    out_specs = (P(None, None, "tile", "frame"), P())
    return jax.shard_map(shards, mesh=mesh, in_specs=in_specs, out_specs=out_specs, check_vma=False)
```

profile of v0, /device:TPU:1, one launch (start us, length us, event | category | flops | bytes accessed | tf_op | source)
XLA Modules:
  0.0 435.5 jit_solution(1999709275929749315)
XLA Ops:
  7.2 0.0 all-gather.3.cloned.1.call-start
  7.2 1.1 fusion.3
  8.3 3.1 collective-permute-start
  11.4 6.1 %collective-permute-done = f32[2,2,128,128]{3,2,1,0:T(8,128)S(1)} collective-permute-done((f32[2,2,128,128]{3,2,1,0:T(8,128)S(1)}, f32[2,2,128,128]{3,2,1,0:T(8,128)S(1)}, u32[]{:S(2)}, u32[]{:S(2)}) %collective-permute-start) | collective-permute-done | bytes 262176 | tf_op jit(solution)/shard_map/ppermute | solution.py:314
  17.5 2.3 collective-permute-done.1
  19.8 2.1 pad_maximum_fusion
  21.9 0.0 all-gather.3.cloned.1.call-update
  22.0 0.0 reduce-scatter.2.cloned.1.call-start
  22.0 109.2 %all-gather.3.cloned.1.call-done = f32[16,2,512,128]{3,2,1,0:T(8,128)} async-done(((f32[2,2,512,128]{3,2,1,0:T(8,128)}), f32[16,2,512,128]{3,2,1,0:T(8,128)}) %all-gather.3.cloned.1.call-update) | async-done | bytes 8388624 | tf_op jit(solution)/shard_map/all_gather | solution.py:322
  131.2 1.4 copy-done
  132.6 1.2 copy-done.1
  133.8 1.0 copy-done.2
  134.8 0.9 copy-done.3
  135.8 0.9 copy-done.4
  136.7 0.9 copy-done.5
  137.7 0.7 copy-done.6
  138.4 24.3 %frame_terms.1 = (f32[8,2,2,512,128]{4,3,2,1,0:T(8,128)}, f32[2,2,256,256]{3,2,1,0:T(8,128)}) custom-call(s32[2,2]{1,0:T(2,128)S(1)} %copy-done.6, f32[8,2,2,512,128]{4,3,2,1,0:T(8,128)} %bitcast.2, f32[2,2,256,256]{3,2,1,0:T(8,128)S(1)} %copy-done.1, f32[256,256]{1,0:T(8,128)S(1)} %copy-done.3, f32[256,256]{1,0:T(8,128)S(1)} %copy-done.4, ...), custom_call_target="tpu_custom_call" | custom-call | tf_op jit(solution)/shard_map/frame_terms/pallas_call | solution.py:284
  162.6 0.0 reduce-scatter.2.cloned.1.call-update
  162.7 0.0 all-reduce.2.cloned.1.call-start
  162.7 112.9 %reduce-scatter.2.cloned.1.call-done = f32[1,2,2,512,128]{4,3,2,1,0:T(8,128)} async-done(((f32[8,2,2,512,128]{4,3,2,1,0:T(8,128)}), f32[1,2,2,512,128]{4,3,2,1,0:T(8,128)}) %reduce-scatter.2.cloned.1.call-update) | async-done | bytes 1048592 | tf_op jit(solution)/shard_map/reduce_scatter | solution.py:325
  275.7 1.1 fusion.2
  276.7 1.3 collective-permute-start.2
  278.0 0.0 all-reduce.2.cloned.1.call-update
  278.0 0.6 collective-permute-start.3
  278.6 1.1 slice.81
  279.7 2.9 collective-permute-done.2
  282.6 1.0 fusion.1
  283.6 1.2 collective-permute-done.3
  284.8 0.1 fusion
  284.8 0.0 copy-start.7
  284.8 141.8 %all-reduce.2.cloned.1.call-done = f32[2,2,256,256]{3,2,1,0:T(8,128)} async-done(((f32[2,2,256,256]{3,2,1,0:T(8,128)}), f32[2,2,256,256]{3,2,1,0:T(8,128)}) %all-reduce.2.cloned.1.call-update) | async-done | bytes 1048592 | tf_op jit(solution)/shard_map/psum | solution.py:324
  426.6 2.3 copy.14
  (9 shorter events, 0.0 us)
Async XLA Ops:
  7.2 124.0 %all-gather.3.cloned.1.call-start = ((), (), s32[]{:S(2)}) async-start(), calls=%async_computation.3 | async-start | bytes 9437184 | tf_op jit(solution)/shard_map/all_gather | solution.py:322
  8.3 9.2 %collective-permute-start = (f32[2,2,128,128]{3,2,1,0:T(8,128)S(1)}, f32[2,2,128,128]{3,2,1,0:T(8,128)S(1)}, u32[]{:S(2)}, u32[]{:S(2)}) collective-permute-start(f32[2,2,128,128]{3,2,1,0:T(8,128)S(1)} %get-tuple-element.32), channel_id=1, source_target_pairs={{0,8},{8,16},{16,24},{24,32},{32,40},{40,48},{48,56},{56,64},{64,7... | collective-permute-start | bytes 786440 | tf_op jit(solution)/shard_map/ppermute | solution.py:314
  11.4 8.5 %collective-permute-start.1 = (f32[2,2,128,128]{3,2,1,0:T(8,128)S(1)}, f32[2,2,128,128]{3,2,1,0:T(8,128)S(1)}, u32[]{:S(2)}, u32[]{:S(2)}) collective-permute-start(f32[2,2,128,128]{3,2,1,0:T(8,128)S(1)} %get-tuple-element.33), channel_id=1, source_target_pairs={{0,120},{8,0},{16,8},{24,16},{32,24},{40,32},{48,40},{56,48},{64,5... | collective-permute-start | bytes 786440 | tf_op jit(solution)/shard_map/ppermute | solution.py:314
  22.0 253.7 %reduce-scatter.2.cloned.1.call-start = ((), (), s32[]{:S(2)}) async-start(), calls=%async_computation.1 | async-start | bytes 9437184 | tf_op jit(solution)/shard_map/reduce_scatter | solution.py:325
  131.2 1.4 copy-start
  132.6 1.2 copy-start.1
  133.8 1.0 copy-start.2
  134.8 0.9 copy-start.3
  135.8 0.9 copy-start.4
  136.7 0.9 copy-start.5
  137.7 0.7 copy-start.6
  162.7 264.0 %all-reduce.2.cloned.1.call-start = ((), (), s32[]{:S(2)}) async-start(), calls=%async_computation.2 | async-start | bytes 2097152 | tf_op jit(solution)/shard_map/psum | solution.py:324
  276.7 5.9 %collective-permute-start.2 = (f32[2,2,128,128]{3,2,1,0:T(8,128)S(1)}, f32[2,2,128,128]{3,2,1,0:T(8,128)S(1)}, u32[]{:S(2)}, u32[]{:S(2)}) collective-permute-start(f32[2,2,128,128]{3,2,1,0:T(8,128)S(1)} %get-tuple-element.31), channel_id=1, source_target_pairs={{0,120},{8,0},{16,8},{24,16},{32,24},{40,32},{48,40},{56,48},{64,5... | collective-permute-start | bytes 786440 | tf_op jit(solution)/shard_map/ppermute | solution.py:314
  278.0 6.7 %collective-permute-start.3 = (f32[2,2,128,128]{3,2,1,0:T(8,128)S(1)}, f32[2,2,128,128]{3,2,1,0:T(8,128)S(1)}, u32[]{:S(2)}, u32[]{:S(2)}) collective-permute-start(f32[2,2,128,128]{3,2,1,0:T(8,128)S(1)} %get-tuple-element.30), channel_id=1, source_target_pairs={{0,8},{8,16},{16,24},{24,32},{32,40},{40,48},{48,56},{56,64},{64,7... | collective-permute-start | bytes 786440 | tf_op jit(solution)/shard_map/ppermute | solution.py:314
  284.8 144.1 %copy-start.7 = (f32[2,2,256,128]{3,2,1,0:T(8,128)}, f32[2,2,256,128]{3,2,1,0:T(8,128)S(1)}, u32[]{:S(2)}) copy-start(f32[2,2,256,128]{3,2,1,0:T(8,128)S(1)} %fusion) | copy-start | bytes 1572868
Sparse Core Ops, SparseCore 0:
  22.1 109.0 all-gather.2
  162.8 112.8 reduce-scatter.1
  281.0 145.5 all-reduce.1
where the time goes:
time: 436 us; the launch traced here: 435 us
  waiting for transfers between devices  376 us (86%)
  Pallas kernels  24.3 us (6%)
  between operations  13.8 us (3%)
  local copies, waits for them, and re-layouts  12.7 us (3%)
  starting transfers between devices  5.1 us (1%)
    psum x1, waiting for transfers between devices, shards(): probe_grad = lax.psum(probe_term, ('tile', 'frame'))  142 us
    reduce_scatter x1, waiting for transfers between devices, shards(): summed = lax.psum_scatter(grads, 'frame', scatter_dimension=0, tiled=False)  113 us
    all_gather x1, waiting for transfers between devices, shards(): ext = lax.all_gather(strip, 'frame', axis=0, tiled=False)  109 us
    pallas_call x1, Pallas kernels, frame_terms(): pl.pallas_call(frame_kernel, out_shape=(jax.ShapeDtypeStruct((STRIPS, SLI...  24.3 us
    ppermute x4, waiting for transfers between devices, shifted(): lax.ppermute(array, axis, [(i, (i + by) % count) for i in range(count)])  12.5 us
    unnamed x17, local copies, waits for them, and re-layouts  9.49 us
  transfers between devices with their start and end apart: 7, of which 7 were waited for; matrix products, arithmetic and copies ran while one was open for 0% of the time, Pallas kernels for 0%

commit v1 on v0

--- a/solution.py
+++ b/solution.py
@@ -1,4 +1,3 @@
-import functools
 import numpy as np
 import ml_dtypes
 import jax
@@ -309,26 +308,281 @@
       jnp.asarray(lefts), jnp.asarray(rights), jnp.asarray(perms))
 
 
-def shifted(array, axis, by):
-    count = lax.axis_size(axis)
-    return lax.ppermute(array, axis, [(i, (i + by) % count) for i in range(count)])
+MESH = pl.DeviceIdType.MESH
+
+
+class Place:
+    def __init__(self):
+        tile, frame = lax.axis_index("tile"), lax.axis_index("frame")
+        self.y, self.zl, self.core = tile // 4, (tile // 2) % 2, tile % 2
+        self.zh, self.x = frame // 4, frame % 4
+        self.z = self.zh * 2 + self.zl
+
+    def at(self, y=None, zl=None, core=None, zh=None, x=None):
+        pick = lambda given, own: own if given is None else given
+        tile = (pick(y, self.y) * 2 + pick(zl, self.zl)) * 2 + pick(core, self.core)
+        return tile, pick(zh, self.zh) * 4 + pick(x, self.x)
+
+    def along_x(self, k):
+        return self.at(x=(self.x + k) % 4)
+
+    def along_y(self, k):
+        return self.at(y=(self.y + k) % 4)
+
+    def in_plane(self, j):
+        q = (self.z * 4 + self.x + j) % 16
+        z = q // 4
+        return q, self.at(zl=z % 2, zh=z // 2, x=q % 4)
+
+    def z_peer(self):
+        return self.at(zh=1 - self.zh)
+
+    def sibling(self):
+        return self.at(core=1 - self.core)
+
+    def outer(self):
+        turn = self.core * self.zl + (1 - self.core) * (1 - self.zl)
+        step = turn * (2 * self.core - 1)
+        zh = turn * (1 - self.zh) + (1 - turn) * self.zh
+        return self.at(y=(self.y + step + 4) % 4, zl=1 - self.zl, core=1 - self.core, zh=zh)
+
+
+def greet(peers):
+    barrier = pltpu.get_barrier_semaphore()
+    for peer in peers:
+        pl.semaphore_signal(barrier, inc=1, device_id=peer, device_id_type=MESH)
+    pl.semaphore_wait(barrier, len(peers))
+
+
+class Sender:
+    def __init__(self, send_sems, recv_sems):
+        self.send_sems, self.recv_sems = send_sems, recv_sems
+        self.started = []
+
+    def copy(self, src, dst, peer):
+        n = len(self.started)
+        made = pltpu.make_async_remote_copy(
+            src_ref=src, dst_ref=dst, send_sem=self.send_sems.at[n], recv_sem=self.recv_sems.at[n],
+            device_id=peer, device_id_type=MESH,
+        )
+        made.start()
+        self.started.append(made)
+        return made
+
+    def finish(self):
+        for made in self.started:
+            made.wait_send()
+
+
+def aligned(row):
+    return pl.multiple_of(row, 8)
+
+
+GATHER_COPIES = 2 * (4 + 3 + 16)
+
+
+def gather_kernel(own_ref, ext_ref, local_sem, send_sems, recv_sems):
+    me = Place()
+    f, zf = me.zh * 4 + me.x, (1 - me.zh) * 4 + me.x
+    sibling, outer, z_peer = me.sibling(), me.outer(), me.z_peer()
+    across = [me.along_x(k) for k in (1, 2, 3)]
+    greet([sibling, outer, z_peer] + across)
+    send = Sender(send_sems, recv_sems)
+    mine = pl.ds(HALO, FRAME)
+    out_src, out_dst = aligned(HALO + HALO * me.core), aligned(384 * (1 - me.core))
+    sib_src, sib_dst = aligned(HALO + HALO * (1 - me.core)), aligned(384 * me.core)
+    edges = []
+
+    def pass_edges(strip, s, ref=None):
+        base = ext_ref.at[strip, s] if ref is None else ref.at[s]
+        shift = 0 if ref is None else HALO
+        edges.append(send.copy(base.at[:, pl.ds(aligned(out_src - shift), HALO), :], ext_ref.at[strip, s, :, pl.ds(out_dst, HALO), :], outer))
+        edges.append(send.copy(base.at[:, pl.ds(aligned(sib_src - shift), HALO), :], ext_ref.at[strip, s, :, pl.ds(sib_dst, HALO), :], sibling))
+
+    keep = pltpu.make_async_copy(own_ref, ext_ref.at[f, :, :, mine, :], local_sem)
+    keep.start()
+    first = {}
+    for s in range(SLICES):
+        first[s, 0] = send.copy(own_ref.at[s], ext_ref.at[f, s, :, mine, :], z_peer)
+        for k in (1, 3, 2):
+            first[s, k] = send.copy(own_ref.at[s], ext_ref.at[f, s, :, mine, :], across[k - 1])
+    for s in range(SLICES):
+        pass_edges(f, s, own_ref)
+    second = {}
+    for s in range(SLICES):
+        first[s, 0].wait_recv()
+        for k in (1, 3, 2):
+            second[s, k] = send.copy(ext_ref.at[zf, s, :, mine, :], ext_ref.at[zf, s, :, mine, :], across[k - 1])
+        pass_edges(zf, s)
+    for batch, half in ((first, me.zh), (second, 1 - me.zh)):
+        for s in range(SLICES):
+            for k in (1, 3, 2):
+                batch[s, k].wait_recv()
+                pass_edges(half * 4 + (me.x + 4 - k) % 4, s)
+    for made in edges:
+        made.wait_recv()
+    keep.wait()
+    send.finish()
+
+
+def gather_windows_rows(own):
+    any_space = pl.BlockSpec(memory_space=pl.ANY)
+    return pl.pallas_call(
+        gather_kernel,
+        out_shape=jax.ShapeDtypeStruct((STRIPS, SLICES, 2, ROWS_EXT, HALF), F32),
+        in_specs=[any_space],
+        out_specs=any_space,
+        scratch_shapes=[
+            pltpu.SemaphoreType.DMA(()),
+            pltpu.SemaphoreType.DMA((GATHER_COPIES,)),
+            pltpu.SemaphoreType.DMA((GATHER_COPIES,)),
+        ],
+        compiler_params=pltpu.CompilerParams(collective_id=1, has_side_effects=True),
+        name="gather_strips",
+    )(own)
+
+
+SCATTER_COPIES = 32 + 12 + 2 + 1 + 3 + 15 + 15 + 3 + 1
+
+
+def scatter_kernel(
+    g_ref, p_ref, out_ref, pout_ref,
+    edge_out, edge_sib, acc, xb, part, zb, sb, ph, yb, pq, xzb, send_sems, recv_sems,
+):
+    me = Place()
+    sibling, outer, z_peer = me.sibling(), me.outer(), me.z_peer()
+    across = [me.along_x(k) for k in (1, 2, 3)]
+    upward = [me.along_y(k) for k in (1, 2, 3)]
+    plane = [me.in_plane(j) for j in range(1, 16)]
+    greet([sibling, outer] + upward + [peer for _, peer in plane])
+    send = Sender(send_sems, recv_sems)
+    out_src, sib_src = aligned(384 * me.core), aligned(384 * (1 - me.core))
+    out_rows, sib_rows = aligned(HALO * me.core), aligned(HALO * (1 - me.core))
+    order = [(s, k) for s in (1, 0) for k in (2, 1, 3, 0)]
+
+    def strip(half, k):
+        return half * 4 + (me.x + k) % 4
+
+    edges = {}
+    for s, k in order:
+        for h in range(2):
+            i = strip(h, k)
+            edges[s, k, h, 0] = send.copy(g_ref.at[i, s, :, pl.ds(out_src, HALO), :], edge_out.at[s, k, h], outer)
+            edges[s, k, h, 1] = send.copy(g_ref.at[i, s, :, pl.ds(sib_src, HALO), :], edge_sib.at[s, k, h], sibling)
+        if (s, k) == order[0]:
+            other = send.copy(p_ref.at[1 - me.core], sb, sibling)
+
+    crossing = {}
+
+    def take_edges(s, k):
+        for h in range(2):
+            edges[s, k, h, 0].wait_recv()
+            edges[s, k, h, 1].wait_recv()
+            i = strip(h, k)
+            for c in range(2):
+                acc[s, k, h, c, pl.ds(out_rows, HALO), :] = (
+                    g_ref[i, s, c, pl.ds(aligned(HALO + out_rows), HALO), :] + edge_out[s, k, h, c]
+                )
+                acc[s, k, h, c, pl.ds(sib_rows, HALO), :] = (
+                    g_ref[i, s, c, pl.ds(aligned(HALO + sib_rows), HALO), :] + edge_sib[s, k, h, c]
+                )
+            if k != 0:
+                crossing[s, k, h] = send.copy(acc.at[s, k, h], xb.at[s, k - 1, h], across[k - 1])
+
+    take_edges(1, 2)
+    other.wait_recv()
+    ph[...] = p_ref[me.core] + sb[...]
+    quarter = lambda y: pl.ds(aligned(64 * y), 64)
+    y_sums = [send.copy(ph.at[:, quarter((me.y + k) % 4), :], yb.at[k - 1], upward[k - 1]) for k in (1, 2, 3)]
+    take_edges(1, 1)
+    take_edges(1, 3)
+    for made in y_sums:
+        made.wait_recv()
+    pq[...] = ph[:, quarter(me.y), :] + yb[0] + yb[1] + yb[2]
+    spot = lambda q: (q // 8, pl.ds(aligned(8 * (q % 8)), 8))
+    plane_sums = []
+    for j, (q, peer) in enumerate(plane):
+        c, rows = spot(q)
+        plane_sums.append(send.copy(pq.at[c, rows, :], xzb.at[j], peer))
+    take_edges(1, 0)
+    take_edges(0, 2)
+    for made in plane_sums:
+        made.wait_recv()
+    q = me.z * 4 + me.x
+    c, rows = spot(q)
+    total = pq[c, rows, :]
+    for j in range(15):
+        total = total + xzb[j]
+    final_rows = pl.ds(aligned(64 * me.y + 8 * (q % 8)), 8)
+    pout_ref[me.core, c, final_rows, :] = total
+    plane_gather = [
+        send.copy(pout_ref.at[me.core, c, final_rows, :], pout_ref.at[me.core, c, final_rows, :], peer)
+        for _, peer in plane
+    ]
+    take_edges(0, 1)
+    take_edges(0, 3)
+    for made in plane_gather:
+        made.wait_recv()
+    mine = pout_ref.at[me.core, :, quarter(me.y), :]
+    y_gather = [send.copy(mine, mine, peer) for peer in upward]
+    take_edges(0, 0)
+
+    last = {}
+    for s in (1, 0):
+        for k in (2, 1, 3):
+            for h in range(2):
+                crossing[s, k, h].wait_recv()
+        for h in range(2):
+            for c in range(2):
+                part[s, h, c] = acc[s, 0, h, c] + xb[s, 0, h, c] + xb[s, 1, h, c] + xb[s, 2, h, c]
+        last[s] = send.copy(part.at[s, 1 - me.zh], zb.at[s], z_peer)
+        if s == 1:
+            for made in y_gather:
+                made.wait_recv()
+            final = send.copy(pout_ref.at[me.core], pout_ref.at[me.core], sibling)
+    for s in (1, 0):
+        last[s].wait_recv()
+        out_ref[s] = part[s, me.zh] + zb[s]
+    final.wait_recv()
+    send.finish()
+
+
+def scatter_sums(grads, probe_term):
+    vmem = pl.BlockSpec(memory_space=pltpu.VMEM)
+    half_strip = (2, HALO, HALF)
+    full_strip = (2, FRAME, HALF)
+    return pl.pallas_call(
+        scatter_kernel,
+        out_shape=(
+            jax.ShapeDtypeStruct((SLICES,) + full_strip, F32),
+            jax.ShapeDtypeStruct((MODES, 2, FRAME, FRAME), F32),
+        ),
+        in_specs=[vmem, vmem],
+        out_specs=(vmem, vmem),
+        scratch_shapes=[
+            pltpu.VMEM((2, 4, 2) + half_strip, F32),
+            pltpu.VMEM((2, 4, 2) + half_strip, F32),
+            pltpu.VMEM((2, 4, 2) + full_strip, F32),
+            pltpu.VMEM((2, 3, 2) + full_strip, F32),
+            pltpu.VMEM((2, 2) + full_strip, F32),
+            pltpu.VMEM((2,) + full_strip, F32),
+            pltpu.VMEM((2, FRAME, FRAME), F32),
+            pltpu.VMEM((2, FRAME, FRAME), F32),
+            pltpu.VMEM((3, 2, 64, FRAME), F32),
+            pltpu.VMEM((2, 64, FRAME), F32),
+            pltpu.VMEM((15, 8, FRAME), F32),
+            pltpu.SemaphoreType.DMA((SCATTER_COPIES,)),
+            pltpu.SemaphoreType.DMA((SCATTER_COPIES,)),
+        ],
+        compiler_params=pltpu.CompilerParams(collective_id=2, has_side_effects=True, vmem_limit_bytes=48 << 20),
+        name="scatter_sums",
+    )(grads, probe_term)
 
 
 def shards(object_slices, probe_modes, prop_phase, background, positions, counts):
-    rows_own = object_slices.shape[2]
-    before = shifted(object_slices[:, :, rows_own - HALO:], "tile", 1)
-    after = shifted(object_slices[:, :, :HALO], "tile", -1)
-    strip = jnp.concatenate([before, object_slices, after], axis=2)
-    ext = lax.all_gather(strip, "frame", axis=0, tiled=False)
+    ext = gather_windows_rows(object_slices)
     grads, probe_term = frame_terms(positions, ext, probe_modes, prop_phase, background, counts)
-    probe_grad = lax.psum(probe_term, ("tile", "frame"))
-    summed = lax.psum_scatter(grads, "frame", scatter_dimension=0, tiled=False)
-    from_below = shifted(summed[:, :, :HALO], "tile", -1)
-    from_above = shifted(summed[:, :, HALO + rows_own:], "tile", 1)
-    object_grad = summed[:, :, HALO:HALO + rows_own]
-    object_grad = object_grad.at[:, :, rows_own - HALO:].add(from_below)
-    object_grad = object_grad.at[:, :, :HALO].add(from_above)
-    return object_grad, probe_grad
+    return scatter_sums(grads, probe_term)
 
 
 def solution(mesh):

time: 436 us -> 159 us (0.36)
  waiting for transfers between devices: 376 us -> 0 us
  Pallas kernels: 24.3 us -> 154 us
  between operations: 13.8 us -> 0.74 us
  local copies, waits for them, and re-layouts: 12.7 us -> 3.68 us
  starting transfers between devices: 5.1 us -> 0 us
    psum x1 -> x0, waiting for transfers between devices: 142 us -> none  [shards(): probe_grad = lax.psum(probe_term, ('tile', 'frame'))]
    pallas_call x0 -> x2, Pallas kernels: none -> 130 us  [the longest x1 70.8 us: scatter_sums(): pl.pallas_call(scatter_kernel, out_shape=(jax.ShapeDtypeStruct((SLICES,)...]
    reduce_scatter x1 -> x0, waiting for transfers between devices: 113 us -> none  [shards(): summed = lax.psum_scatter(grads, 'frame', scatter_dimension=0, tiled=False)]
    all_gather x1 -> x0, waiting for transfers between devices: 109 us -> none  [shards(): ext = lax.all_gather(strip, 'frame', axis=0, tiled=False)]
    ppermute x4 -> x0, waiting for transfers between devices: 12.5 us -> none  [shifted(): lax.ppermute(array, axis, [(i, (i + by) % count) for i in range(count)])]
    unnamed x17 -> x16, local copies, waits for them, and re-layouts: 9.49 us -> 3.68 us
    ppermute x4 -> x0, starting transfers between devices: 4.98 us -> none  [shifted(): lax.ppermute(array, axis, [(i, (i + by) % count) for i in range(count)])]
  transfers between devices with their start and end apart: 7 -> 0, of which waited for: 7 -> 0; matrix products, arithmetic and copies ran while one was open for 0% -> 0% of each run, Pallas kernels for 0% -> 0%
where the time goes in v1:
time: 159 us
  Pallas kernels  154 us (97%)
  local copies, waits for them, and re-layouts  3.68 us (2%)
    pallas_call x1, Pallas kernels, scatter_sums(): pl.pallas_call(scatter_kernel, out_shape=(jax.ShapeDtypeStruct((SLICES,)...  70.8 us
    pallas_call x1, Pallas kernels, gather_windows_rows(): pl.pallas_call(gather_kernel, out_shape=jax.ShapeDtypeStruct((STRIPS, SLI...  59.7 us
    pallas_call x1, Pallas kernels, frame_terms(): pl.pallas_call(frame_kernel, out_shape=(jax.ShapeDtypeStruct((STRIPS, SLI...  23.9 us
    unnamed x16, local copies, waits for them, and re-layouts  3.68 us

profile of v1, /device:TPU:1, one launch (start us, length us, event | category | flops | bytes accessed | tf_op | source)
XLA Modules:
  0.0 158.9 jit_solution(15788808375664025839)
XLA Ops:
  0.6 0.0 copy-start
  0.6 0.0 copy-start.2
  0.7 0.0 copy-start.6
  0.7 0.0 copy-start.3
  0.7 0.0 copy-start.1
  0.7 59.7 %gather_strips.1.ext_ref = f32[8,2,2,512,128]{4,3,2,1,0:T(8,128)} custom-call(f32[2,2,256,128]{3,2,1,0:T(8,128)} %own_ref.1), custom_call_target="tpu_custom_call" | custom-call | tf_op jit(solution)/shard_map/gather_strips/pallas_call | solution.py:430
  60.4 0.0 copy-done
  60.4 0.0 copy-done.2
  60.4 0.0 copy-done.6
  60.4 0.0 copy-done.3
  60.4 0.0 copy-done.1
  60.4 0.0 copy-start.4
  60.4 0.9 copy-done.4
  61.4 0.0 copy-start.5
  61.4 0.9 copy-done.5
  62.3 23.9 %frame_terms.1 = (f32[8,2,2,512,128]{4,3,2,1,0:T(8,128)}, f32[2,2,256,256]{3,2,1,0:T(8,128)S(1)}) custom-call(s32[2,2]{1,0:T(2,128)S(1)} %copy-done.6, f32[8,2,2,512,128]{4,3,2,1,0:T(8,128)} %gather_strips.1.ext_ref, f32[2,2,256,256]{3,2,1,0:T(8,128)S(1)} %copy-done.1, f32[256,256]{1,0:T(8,128)S(1)} %copy-done.3, f32[256,256]{1,0:T(8,128)S(1)} %copy-done.4, ...), custom_call_target="tpu_custom_call" | custom-call | tf_op jit(solution)/shard_map/frame_terms/pallas_call | solution.py:283
  86.2 70.8 %scatter_sums.1 = (f32[2,2,256,128]{3,2,1,0:T(8,128)S(1)}, f32[2,2,256,256]{3,2,1,0:T(8,128)S(1)}) custom-call(f32[8,2,2,512,128]{4,3,2,1,0:T(8,128)} %get-tuple-element.4.g_ref, f32[2,2,256,256]{3,2,1,0:T(8,128)S(1)} %get-tuple-element.5.p_ref), custom_call_target="tpu_custom_call" | custom-call | tf_op jit(solution)/shard_map/scatter_sums/pallas_call | solution.py:554
  157.1 0.8 copy.13
  157.9 1.0 copy.14
Async XLA Ops:
  0.6 59.7 %copy-start = (bf16[4,256,768]{2,1,0:T(8,128)(2,1)S(1)}, bf16[4,256,768]{2,1,0:T(8,128)(2,1)}, u32[]{:S(2)}) copy-start(bf16[4,256,768]{2,1,0:T(8,128)(2,1)} %constant.6.clone.left_ref) | copy-start | bytes 4718596
  0.6 59.7 %copy-start.2 = (s32[2,256,256]{2,1,0:T(8,128)S(1)}, s32[2,256,256]{2,1,0:T(8,128)}, u32[]{:S(2)}) copy-start(s32[2,256,256]{2,1,0:T(8,128)} %counts_ref.1) | copy-start | bytes 1572868
  0.7 59.7 %copy-start.6 = (s32[2,2]{1,0:T(2,128)S(1)}, s32[2,2]{1,0:T(2,128)}, u32[]{:S(2)}) copy-start(s32[2,2]{1,0:T(2,128)} %pos_ref.1) | copy-start | bytes 52
  0.7 59.7 %copy-start.3 = (f32[256,256]{1,0:T(8,128)S(1)}, f32[256,256]{1,0:T(8,128)}, u32[]{:S(2)}) copy-start(f32[256,256]{1,0:T(8,128)} %phase_ref.1) | copy-start | bytes 786436
  0.7 59.7 %copy-start.1 = (f32[2,2,256,256]{3,2,1,0:T(8,128)S(1)}, f32[2,2,256,256]{3,2,1,0:T(8,128)}, u32[]{:S(2)}) copy-start(f32[2,2,256,256]{3,2,1,0:T(8,128)} %probe_ref.1) | copy-start | bytes 3145732
  60.4 1.0 copy-start.4
  61.4 0.9 copy-start.5

commit v2 on v1

--- a/solution.py
+++ b/solution.py
@@ -378,15 +378,15 @@
     return pl.multiple_of(row, 8)
 
 
-GATHER_COPIES = 2 * (4 + 3 + 16)
+GATHER_COPIES = 6 + 4 + 8 + 32
 
 
 def gather_kernel(own_ref, ext_ref, local_sem, send_sems, recv_sems):
     me = Place()
     f, zf = me.zh * 4 + me.x, (1 - me.zh) * 4 + me.x
     sibling, outer, z_peer = me.sibling(), me.outer(), me.z_peer()
-    across = [me.along_x(k) for k in (1, 2, 3)]
-    greet([sibling, outer, z_peer] + across)
+    ahead, behind = me.along_x(1), me.along_x(3)
+    greet([sibling, outer, z_peer, ahead, behind])
     send = Sender(send_sems, recv_sems)
     mine = pl.ds(HALO, FRAME)
     out_src, out_dst = aligned(HALO + HALO * me.core), aligned(384 * (1 - me.core))
@@ -401,24 +401,50 @@
 
     keep = pltpu.make_async_copy(own_ref, ext_ref.at[f, :, :, mine, :], local_sem)
     keep.start()
-    first = {}
+    to_z, to_x, relayed = {}, {}, {}
+    own_half, other_half = 0, 1
+    half_of = (me.zh, 1 - me.zh)
+
+    def strip_at(which, k):
+        return half_of[which] * 4 + (me.x + k + 4) % 4
+
     for s in range(SLICES):
-        first[s, 0] = send.copy(own_ref.at[s], ext_ref.at[f, s, :, mine, :], z_peer)
-        for k in (1, 3, 2):
-            first[s, k] = send.copy(own_ref.at[s], ext_ref.at[f, s, :, mine, :], across[k - 1])
+        to_z[s] = send.copy(own_ref.at[s], ext_ref.at[f, s, :, mine, :], z_peer)
+        to_x[own_half, s, 0] = send.copy(own_ref.at[s], ext_ref.at[f, s, :, mine, :], ahead)
+        to_x[own_half, s, 1] = send.copy(own_ref.at[s], ext_ref.at[f, s, :, mine, :], behind)
     for s in range(SLICES):
         pass_edges(f, s, own_ref)
-    second = {}
-    for s in range(SLICES):
-        first[s, 0].wait_recv()
-        for k in (1, 3, 2):
-            second[s, k] = send.copy(ext_ref.at[zf, s, :, mine, :], ext_ref.at[zf, s, :, mine, :], across[k - 1])
+
+    def from_z(s):
+        to_z[s].wait_recv()
+        whole = ext_ref.at[zf, s, :, mine, :]
+        to_x[other_half, s, 0] = send.copy(whole, whole, ahead)
+        to_x[other_half, s, 1] = send.copy(whole, whole, behind)
         pass_edges(zf, s)
-    for batch, half in ((first, me.zh), (second, 1 - me.zh)):
-        for s in range(SLICES):
-            for k in (1, 3, 2):
-                batch[s, k].wait_recv()
-                pass_edges(half * 4 + (me.x + 4 - k) % 4, s)
+
+    def from_x(which, s):
+        for way, peer, k in ((0, ahead, -1), (1, behind, 1)):
+            to_x[which, s, way].wait_recv()
+            plane = ext_ref.at[strip_at(which, k), s, way, mine, :]
+            relayed[which, s, way] = send.copy(plane, plane, peer)
+        for k in (-1, 1):
+            pass_edges(strip_at(which, k), s)
+
+    def from_relay(which, s):
+        for way in range(2):
+            relayed[which, s, way].wait_recv()
+        pass_edges(strip_at(which, 2), s)
+
+    from_z(0)
+    from_x(own_half, 0)
+    from_z(1)
+    from_x(own_half, 1)
+    from_relay(own_half, 0)
+    from_x(other_half, 0)
+    from_relay(own_half, 1)
+    from_x(other_half, 1)
+    from_relay(other_half, 0)
+    from_relay(other_half, 1)
     for made in edges:
         made.wait_recv()
     keep.wait()
@@ -442,52 +468,74 @@
     )(own)
 
 
-SCATTER_COPIES = 32 + 12 + 2 + 1 + 3 + 15 + 15 + 3 + 1
+SCATTER_COPIES = 32 + 8 + 16 + 2 + 1 + 3 + 15 + 15 + 3 + 1
 
 
 def scatter_kernel(
     g_ref, p_ref, out_ref, pout_ref,
-    edge_out, edge_sib, acc, xb, part, zb, sb, ph, yb, pq, xzb, send_sems, recv_sems,
+    edge_out, edge_sib, acc, rb, xb, part, zb, sb, ph, yb, pq, xzb, local_sems, send_sems, recv_sems,
 ):
     me = Place()
     sibling, outer, z_peer = me.sibling(), me.outer(), me.z_peer()
-    across = [me.along_x(k) for k in (1, 2, 3)]
+    ahead, behind = me.along_x(1), me.along_x(3)
     upward = [me.along_y(k) for k in (1, 2, 3)]
     plane = [me.in_plane(j) for j in range(1, 16)]
     greet([sibling, outer] + upward + [peer for _, peer in plane])
     send = Sender(send_sems, recv_sems)
     out_src, sib_src = aligned(384 * me.core), aligned(384 * (1 - me.core))
     out_rows, sib_rows = aligned(HALO * me.core), aligned(HALO * (1 - me.core))
-    order = [(s, k) for s in (1, 0) for k in (2, 1, 3, 0)]
+    order = [(1, 2), (1, 1), (1, 3), (0, 2), (0, 1), (0, 3), (1, 0), (0, 0)]
 
     def strip(half, k):
         return half * 4 + (me.x + k) % 4
 
+    local = {}
+    for n, (s, k) in enumerate(order):
+        for h in range(2):
+            local[s, k, h] = pltpu.make_async_copy(
+                g_ref.at[strip(h, k), s, :, pl.ds(HALO, FRAME), :], acc.at[s, k, h], local_sems.at[n, h]
+            )
+            local[s, k, h].start()
     edges = {}
-    for s, k in order:
-        for h in range(2):
-            i = strip(h, k)
-            edges[s, k, h, 0] = send.copy(g_ref.at[i, s, :, pl.ds(out_src, HALO), :], edge_out.at[s, k, h], outer)
-            edges[s, k, h, 1] = send.copy(g_ref.at[i, s, :, pl.ds(sib_src, HALO), :], edge_sib.at[s, k, h], sibling)
-        if (s, k) == order[0]:
-            other = send.copy(p_ref.at[1 - me.core], sb, sibling)
-
-    crossing = {}
+    waiting = list(order)
+
+    def start_edges():
+        if waiting:
+            s, k = waiting.pop(0)
+            for h in range(2):
+                i = strip(h, k)
+                edges[s, k, h, 0] = send.copy(g_ref.at[i, s, :, pl.ds(out_src, HALO), :], edge_out.at[s, k, h], outer)
+                edges[s, k, h, 1] = send.copy(g_ref.at[i, s, :, pl.ds(sib_src, HALO), :], edge_sib.at[s, k, h], sibling)
+
+    start_edges()
+    start_edges()
+    other = send.copy(p_ref.at[1 - me.core], sb, sibling)
+    start_edges()
+    relays, crossing = {}, {}
 
     def take_edges(s, k):
         for h in range(2):
+            local[s, k, h].wait()
             edges[s, k, h, 0].wait_recv()
             edges[s, k, h, 1].wait_recv()
-            i = strip(h, k)
-            for c in range(2):
-                acc[s, k, h, c, pl.ds(out_rows, HALO), :] = (
-                    g_ref[i, s, c, pl.ds(aligned(HALO + out_rows), HALO), :] + edge_out[s, k, h, c]
-                )
-                acc[s, k, h, c, pl.ds(sib_rows, HALO), :] = (
-                    g_ref[i, s, c, pl.ds(aligned(HALO + sib_rows), HALO), :] + edge_sib[s, k, h, c]
-                )
-            if k != 0:
-                crossing[s, k, h] = send.copy(acc.at[s, k, h], xb.at[s, k - 1, h], across[k - 1])
+            acc[s, k, h, :, pl.ds(out_rows, HALO), :] += edge_out[s, k, h]
+            acc[s, k, h, :, pl.ds(sib_rows, HALO), :] += edge_sib[s, k, h]
+        for h in range(2):
+            if k == 2:
+                relays[s, h, 0] = send.copy(acc.at[s, k, h, 0], rb.at[s, h, 0], ahead)
+                relays[s, h, 1] = send.copy(acc.at[s, k, h, 1], rb.at[s, h, 1], behind)
+            if k == 1:
+                crossing[s, h, 0, 1] = send.copy(acc.at[s, k, h, 1], xb.at[s, h, 0, 1], ahead)
+            if k == 3:
+                crossing[s, h, 1, 0] = send.copy(acc.at[s, k, h, 0], xb.at[s, h, 1, 0], behind)
+        start_edges()
+
+    def take_relays(s):
+        for h in range(2):
+            for way, k, peer in ((0, 1, ahead), (1, 3, behind)):
+                relays[s, h, way].wait_recv()
+                acc[s, k, h, way] += rb[s, h, way]
+                crossing[s, h, way, way] = send.copy(acc.at[s, k, h, way], xb.at[s, h, way, way], peer)
 
     take_edges(1, 2)
     other.wait_recv()
@@ -504,7 +552,7 @@
     for j, (q, peer) in enumerate(plane):
         c, rows = spot(q)
         plane_sums.append(send.copy(pq.at[c, rows, :], xzb.at[j], peer))
-    take_edges(1, 0)
+    take_relays(1)
     take_edges(0, 2)
     for made in plane_sums:
         made.wait_recv()
@@ -521,6 +569,8 @@
     ]
     take_edges(0, 1)
     take_edges(0, 3)
+    take_relays(0)
+    take_edges(1, 0)
     for made in plane_gather:
         made.wait_recv()
     mine = pout_ref.at[me.core, :, quarter(me.y), :]
@@ -529,12 +579,11 @@
 
     last = {}
     for s in (1, 0):
-        for k in (2, 1, 3):
-            for h in range(2):
-                crossing[s, k, h].wait_recv()
         for h in range(2):
-            for c in range(2):
-                part[s, h, c] = acc[s, 0, h, c] + xb[s, 0, h, c] + xb[s, 1, h, c] + xb[s, 2, h, c]
+            for way in range(2):
+                for c in range(2):
+                    crossing[s, h, way, c].wait_recv()
+            part[s, h] = acc[s, 0, h] + xb[s, h, 0] + xb[s, h, 1]
         last[s] = send.copy(part.at[s, 1 - me.zh], zb.at[s], z_peer)
         if s == 1:
             for made in y_gather:
@@ -557,13 +606,14 @@
             jax.ShapeDtypeStruct((SLICES,) + full_strip, F32),
             jax.ShapeDtypeStruct((MODES, 2, FRAME, FRAME), F32),
         ),
-        in_specs=[vmem, vmem],
+        in_specs=[pl.BlockSpec(memory_space=pl.ANY), vmem],
         out_specs=(vmem, vmem),
         scratch_shapes=[
             pltpu.VMEM((2, 4, 2) + half_strip, F32),
             pltpu.VMEM((2, 4, 2) + half_strip, F32),
             pltpu.VMEM((2, 4, 2) + full_strip, F32),
-            pltpu.VMEM((2, 3, 2) + full_strip, F32),
+            pltpu.VMEM((2, 2, 2, FRAME, HALF), F32),
+            pltpu.VMEM((2, 2, 2) + full_strip, F32),
             pltpu.VMEM((2, 2) + full_strip, F32),
             pltpu.VMEM((2,) + full_strip, F32),
             pltpu.VMEM((2, FRAME, FRAME), F32),
@@ -571,6 +621,7 @@
             pltpu.VMEM((3, 2, 64, FRAME), F32),
             pltpu.VMEM((2, 64, FRAME), F32),
             pltpu.VMEM((15, 8, FRAME), F32),
+            pltpu.SemaphoreType.DMA((8, 2)),
             pltpu.SemaphoreType.DMA((SCATTER_COPIES,)),
             pltpu.SemaphoreType.DMA((SCATTER_COPIES,)),
         ],

time: 159 us -> 138 us (0.87)
  Pallas kernels: 154 us -> 134 us
    pallas_call x1, Pallas kernels: 59.7 us -> 48.4 us  [gather_windows_rows(): pl.pallas_call(gather_kernel, out_shape=jax.ShapeDtypeStruct((STRIPS, SLI...]
    pallas_call x1, Pallas kernels: 70.8 us -> 61.4 us  [scatter_sums(): pl.pallas_call(scatter_kernel, out_shape=(jax.ShapeDtypeStruct((SLICES,)...]
where the time goes in v2:
time: 138 us
  Pallas kernels  134 us (97%)
  local copies, waits for them, and re-layouts  3.68 us (3%)
    pallas_call x1, Pallas kernels, scatter_sums(): pl.pallas_call(scatter_kernel, out_shape=(jax.ShapeDtypeStruct((SLICES,)...  61.4 us
    pallas_call x1, Pallas kernels, gather_windows_rows(): pl.pallas_call(gather_kernel, out_shape=jax.ShapeDtypeStruct((STRIPS, SLI...  48.4 us
    pallas_call x1, Pallas kernels, frame_terms(): pl.pallas_call(frame_kernel, out_shape=(jax.ShapeDtypeStruct((STRIPS, SLI...  23.9 us
    unnamed x16, local copies, waits for them, and re-layouts  3.68 us

profile of v2, /device:TPU:1, one launch (start us, length us, event | category | flops | bytes accessed | tf_op | source)
XLA Modules:
  0.0 138.1 jit_solution(10395472115578924650)
XLA Ops:
  0.6 0.0 copy-start
  0.6 0.0 copy-start.2
  0.7 0.0 copy-start.6
  0.7 0.0 copy-start.3
  0.7 0.0 copy-start.1
  0.7 48.4 %gather_strips.1.ext_ref = f32[8,2,2,512,128]{4,3,2,1,0:T(8,128)} custom-call(f32[2,2,256,128]{3,2,1,0:T(8,128)} %own_ref.1), custom_call_target="tpu_custom_call" | custom-call | tf_op jit(solution)/shard_map/gather_strips/pallas_call | solution.py:456
  49.1 0.0 copy-done
  49.1 0.0 copy-done.2
  49.1 0.0 copy-done.6
  49.1 0.0 copy-done.3
  49.1 0.0 copy-done.1
  49.1 0.0 copy-start.4
  49.1 0.9 copy-done.4
  50.1 0.0 copy-start.5
  50.1 0.9 copy-done.5
  51.0 23.9 %frame_terms.1 = (f32[8,2,2,512,128]{4,3,2,1,0:T(8,128)}, f32[2,2,256,256]{3,2,1,0:T(8,128)S(1)}) custom-call(s32[2,2]{1,0:T(2,128)S(1)} %copy-done.6, f32[8,2,2,512,128]{4,3,2,1,0:T(8,128)} %gather_strips.1.ext_ref, f32[2,2,256,256]{3,2,1,0:T(8,128)S(1)} %copy-done.1, f32[256,256]{1,0:T(8,128)S(1)} %copy-done.3, f32[256,256]{1,0:T(8,128)S(1)} %copy-done.4, ...), custom_call_target="tpu_custom_call" | custom-call | tf_op jit(solution)/shard_map/frame_terms/pallas_call | solution.py:283
  74.9 61.4 %scatter_sums.1 = (f32[2,2,256,128]{3,2,1,0:T(8,128)S(1)}, f32[2,2,256,256]{3,2,1,0:T(8,128)S(1)}) custom-call(f32[8,2,2,512,128]{4,3,2,1,0:T(8,128)} %get-tuple-element.4.g_ref, f32[2,2,256,256]{3,2,1,0:T(8,128)S(1)} %get-tuple-element.5.p_ref), custom_call_target="tpu_custom_call" | custom-call | tf_op jit(solution)/shard_map/scatter_sums/pallas_call | solution.py:603
  136.3 0.8 copy.13
  137.1 1.0 copy.14
Async XLA Ops:
  0.6 48.4 %copy-start = (bf16[4,256,768]{2,1,0:T(8,128)(2,1)S(1)}, bf16[4,256,768]{2,1,0:T(8,128)(2,1)}, u32[]{:S(2)}) copy-start(bf16[4,256,768]{2,1,0:T(8,128)(2,1)} %constant.6.clone.left_ref) | copy-start | bytes 4718596
  0.6 48.4 %copy-start.2 = (s32[2,256,256]{2,1,0:T(8,128)S(1)}, s32[2,256,256]{2,1,0:T(8,128)}, u32[]{:S(2)}) copy-start(s32[2,256,256]{2,1,0:T(8,128)} %counts_ref.1) | copy-start | bytes 1572868
  0.7 48.4 %copy-start.6 = (s32[2,2]{1,0:T(2,128)S(1)}, s32[2,2]{1,0:T(2,128)}, u32[]{:S(2)}) copy-start(s32[2,2]{1,0:T(2,128)} %pos_ref.1) | copy-start | bytes 52
  0.7 48.4 %copy-start.3 = (f32[256,256]{1,0:T(8,128)S(1)}, f32[256,256]{1,0:T(8,128)}, u32[]{:S(2)}) copy-start(f32[256,256]{1,0:T(8,128)} %phase_ref.1) | copy-start | bytes 786436
  0.7 48.4 %copy-start.1 = (f32[2,2,256,256]{3,2,1,0:T(8,128)S(1)}, f32[2,2,256,256]{3,2,1,0:T(8,128)}, u32[]{:S(2)}) copy-start(f32[2,2,256,256]{3,2,1,0:T(8,128)} %probe_ref.1) | copy-start | bytes 3145732
  49.1 1.0 copy-start.4
  50.1 0.9 copy-start.5

commit v3 on v0

v3 whole, which is shorter than its diff:
```python
import numpy as np
import ml_dtypes
import jax
import jax.numpy as jnp
from jax import lax
from jax.experimental import pallas as pl
from jax.experimental.pallas import tpu as pltpu
from jax.sharding import PartitionSpec as P

FRAME = 256
HALF = 128
SLICES = 2
MODES = 2
HALO = 128
ROWS_EXT = 512
STRIPS = 8
WIN_COLS = 384
CHUNK = 32
TALL = 88
BLANK_ROWS = 248
PAD_ROWS = 2 * BLANK_ROWS + 264
F32 = jnp.float32
BF16 = jnp.bfloat16


def dft_constants():
    k = np.arange(HALF)[:, None]
    n = np.arange(HALF)[None, :]
    mats = []
    for odd in (0, 1):
        turns = ((2 * k + odd) * n) % FRAME
        angle = -2.0 * np.pi * turns / FRAME
        c, s = np.cos(angle) / 16.0, np.sin(angle) / 16.0
        mats.append(np.block([[c, -s], [s, c]]))
    even, odd = mats
    lefts, rights = [], []
    for m in (even, odd, even.T, odd.T):
        hi = m.astype(ml_dtypes.bfloat16)
        lo = (m - hi.astype(np.float64)).astype(ml_dtypes.bfloat16)
        lefts.append(np.concatenate([hi, hi, lo], axis=1))
        rights.append(np.concatenate([hi, hi, lo], axis=0))
    perm = np.zeros((FRAME, FRAME))
    order = np.concatenate([np.arange(0, FRAME, 2), np.arange(1, FRAME, 2)])
    perm[np.arange(FRAME), order] = 1.0
    perms = np.stack([perm, perm.T]).astype(ml_dtypes.bfloat16)
    return np.stack(lefts), np.stack(rights), perms


def mm(a, b):
    return jnp.dot(a, b, preferred_element_type=F32)


def parts3(x):
    a = x.astype(BF16)
    r = x - a.astype(F32)
    b = r.astype(BF16)
    c = (r - b.astype(F32)).astype(BF16)
    return a, b, c


def reorder_exact(x, perm, perm_t):
    a, b, c = parts3(x)
    y = mm(perm, a) + mm(perm, b) + mm(perm, c)
    a, b, c = parts3(y)
    return mm(a, perm_t) + mm(b, perm_t) + mm(c, perm_t)


def corner(pos_ref, f):
    r, c = pos_ref[f, 0], pos_ref[f, 1]
    block = jnp.minimum(r // 8, 31)
    cs = jnp.minimum(c // HALF, 5)
    return block, r - block * 8, cs, c - cs * HALF


MESH = pl.DeviceIdType.MESH


class Place:
    def __init__(self):
        tile, frame = lax.axis_index("tile"), lax.axis_index("frame")
        self.y, self.zl, self.core = tile // 4, (tile // 2) % 2, tile % 2
        self.zh, self.x = frame // 4, frame % 4
        self.z = self.zh * 2 + self.zl

    def at(self, y=None, zl=None, core=None, zh=None, x=None):
        pick = lambda given, own: own if given is None else given
        tile = (pick(y, self.y) * 2 + pick(zl, self.zl)) * 2 + pick(core, self.core)
        return tile, pick(zh, self.zh) * 4 + pick(x, self.x)

    def along_x(self, k):
        return self.at(x=(self.x + k) % 4)

    def along_y(self, k):
        return self.at(y=(self.y + k) % 4)

    def in_plane(self, j):
        q = (self.z * 4 + self.x + j) % 16
        z = q // 4
        return q, self.at(zl=z % 2, zh=z // 2, x=q % 4)

    def z_peer(self):
        return self.at(zh=1 - self.zh)

    def sibling(self):
        return self.at(core=1 - self.core)

    def outer(self):
        turn = self.core * self.zl + (1 - self.core) * (1 - self.zl)
        step = turn * (2 * self.core - 1)
        zh = turn * (1 - self.zh) + (1 - turn) * self.zh
        return self.at(y=(self.y + step + 4) % 4, zl=1 - self.zl, core=1 - self.core, zh=zh)


def greet(peers):
    barrier = pltpu.get_barrier_semaphore()
    for peer in peers:
        pl.semaphore_signal(barrier, inc=1, device_id=peer, device_id_type=MESH)
    pl.semaphore_wait(barrier, len(peers))


class Sender:
    def __init__(self, send_sems, recv_sems):
        self.send_sems, self.recv_sems = send_sems, recv_sems
        self.started = []

    def copy(self, src, dst, peer):
        n = len(self.started)
        made = pltpu.make_async_remote_copy(
            src_ref=src, dst_ref=dst, send_sem=self.send_sems.at[n], recv_sem=self.recv_sems.at[n],
            device_id=peer, device_id_type=MESH,
        )
        made.start()
        self.started.append(made)
        return made

    def finish(self):
        for made in self.started:
            made.wait_send()


def aligned(row):
    return pl.multiple_of(row, 8)


GATHER_COPIES = 6 + 4 + 8 + 32
SCATTER_COPIES = 32 + 8 + 16 + 2 + 1 + 3 + 15 + 15 + 3 + 1
COPIES = GATHER_COPIES + SCATTER_COPIES


def gradient_kernel(
    pos_ref, own_ref, probe_in, phase_in, back_in, counts_in, left_in, right_in, perm_in,
    out_ref, pout_ref,
    ext_0, ext_1, g_0, g_1, probe, phase_raw, back_raw, counts_raw, left, right, perms,
    obj, kern, bg, cnt, wave, u1, rop, lop, tmp, freq, padded, placed,
    edge_out, edge_sib, rb, xb, part, zb, p_sum, sb, ph, yb, pq, xzb,
    local_sems, send_sems, recv_sems,
):
    exts, gs = (ext_0, ext_1), (g_0, g_1)
    me = Place()
    f_own, f_other = me.zh * 4 + me.x, (1 - me.zh) * 4 + me.x
    sibling, outer, z_peer = me.sibling(), me.outer(), me.z_peer()
    ahead, behind = me.along_x(1), me.along_x(3)
    upward = [me.along_y(k) for k in (1, 2, 3)]
    plane = [me.in_plane(j) for j in range(1, 16)]

    loads = [
        pltpu.make_async_copy(src, dst, local_sems.at[n])
        for n, (src, dst) in enumerate((
            (perm_in, perms), (back_in, back_raw), (phase_in, phase_raw), (counts_in, counts_raw),
            (probe_in, probe), (left_in, left), (right_in, right),
        ))
    ]
    for load in loads:
        load.start()
    mine, own_blocks = pl.ds(HALO, FRAME), pl.ds(16, 32)
    keeps = [
        pltpu.make_async_copy(own_ref.at[s], exts[s].at[f_own, :, own_blocks], local_sems.at[len(loads) + s])
        for s in range(SLICES)
    ]
    for keep in keeps:
        keep.start()

    greet([sibling, outer] + upward + [peer for _, peer in plane])
    send = Sender(send_sems, recv_sems)

    out_src, out_dst = 16 + 16 * me.core, 48 * (1 - me.core)
    sib_src, sib_dst = 16 + 16 * (1 - me.core), 48 * me.core
    margins = ([], [])

    def pass_edges(strip, s, ref=None):
        base = exts[s].at[strip] if ref is None else ref.at[s]
        shift = 0 if ref is None else 16
        for src, dst, peer in ((out_src, out_dst, outer), (sib_src, sib_dst, sibling)):
            margins[s].append(send.copy(
                base.at[:, pl.ds(src - shift, 16)], exts[s].at[strip, :, pl.ds(dst, 16)], peer
            ))

    to_z, to_x, relayed = {}, {}, {}
    own_half, other_half = 0, 1
    half_of = (me.zh, 1 - me.zh)

    def strip_at(which, k):
        return half_of[which] * 4 + (me.x + k + 4) % 4

    def own_to_z(s):
        to_z[s] = send.copy(own_ref.at[s], exts[s].at[f_own, :, own_blocks], z_peer)

    def own_to_x(s):
        to_x[own_half, s, 0] = send.copy(own_ref.at[s], exts[s].at[f_own, :, own_blocks], ahead)
        to_x[own_half, s, 1] = send.copy(own_ref.at[s], exts[s].at[f_own, :, own_blocks], behind)

    def from_z(s):
        to_z[s].wait_recv()
        whole = exts[s].at[f_other, :, own_blocks]
        to_x[other_half, s, 0] = send.copy(whole, whole, ahead)
        to_x[other_half, s, 1] = send.copy(whole, whole, behind)
        pass_edges(f_other, s)

    def from_x(which, s):
        for way, peer, k in ((0, ahead, -1), (1, behind, 1)):
            to_x[which, s, way].wait_recv()
            half = exts[s].at[strip_at(which, k), way, own_blocks]
            relayed[which, s, way] = send.copy(half, half, peer)
        for k in (-1, 1):
            pass_edges(strip_at(which, k), s)

    def from_relay(which, s):
        for way in range(2):
            relayed[which, s, way].wait_recv()
        pass_edges(strip_at(which, 2), s)

    def cut(s):
        keeps[s].wait()
        for made in margins[s]:
            made.wait_recv()

        @pl.loop(0, 2)
        def _(f):
            block, row_shift, cs, col_shift = corner(pos_ref, f)
            for p in range(2):
                for q in range(FRAME // CHUNK):
                    x = jnp.concatenate([
                        jnp.concatenate([exts[s][cs + j, p, block + q * CHUNK // 8 + n] for n in range(CHUNK // 8 + 1)], axis=0)
                        for j in range(3)
                    ], axis=1)
                    x = pltpu.roll(x, lax.rem(WIN_COLS - col_shift, WIN_COLS), 1)[:, :FRAME]
                    x = pltpu.roll(x, lax.rem(CHUNK + 8 - row_shift, CHUNK + 8), 0)
                    obj[f, s, p, pl.ds(q * CHUNK, CHUNK), :] = x[:CHUNK]

    def put_right(m, parity, rows, x):
        hi = x.astype(BF16)
        lo = (x - hi.astype(F32)).astype(BF16)
        rop[m, parity, rows, 0:256] = hi
        rop[m, parity, rows, 256:512] = lo
        rop[m, parity, rows, 512:768] = hi

    def put_left(m, parity, start, x):
        hi = x.astype(BF16)
        lo = (x - hi.astype(F32)).astype(BF16)
        n = x.shape[0]
        lop[m, parity, pl.ds(start, n), :] = hi
        lop[m, parity, pl.ds(256 + start, n), :] = lo
        lop[m, parity, pl.ds(512 + start, n), :] = hi

    def forward(m, produce):
        for q in range(FRAME // CHUNK):
            rows = pl.ds(q * CHUNK, CHUNK)
            re, im = produce(m, rows)
            a, b = re[:, :HALF], re[:, HALF:]
            c, d = im[:, :HALF], im[:, HALF:]
            put_right(m, 0, rows, jnp.concatenate([a + b, c + d], axis=1))
            put_right(m, 1, rows, jnp.concatenate([a - b, c - d], axis=1))
        tmp[m, 0] = mm(rop[m, 0], right[2])
        tmp[m, 1] = mm(rop[m, 1], right[3])
        for q in range(HALF // CHUNK):
            top = pl.ds(q * CHUNK, CHUNK)
            bot = pl.ds(HALF + q * CHUNK, CHUNK)
            et, eb = tmp[m, 0, top, :], tmp[m, 0, bot, :]
            ot, ob = tmp[m, 1, top, :], tmp[m, 1, bot, :]
            for parity, e, o in ((0, et + eb, ot + ob), (1, et - eb, ot - ob)):
                put_left(m, parity, q * CHUNK, jnp.concatenate([e[:, :HALF], o[:, :HALF]], axis=1))
                put_left(m, parity, HALF + q * CHUNK, jnp.concatenate([e[:, HALF:], o[:, HALF:]], axis=1))
        freq[m, 0] = mm(left[0], lop[m, 0])
        freq[m, 1] = mm(left[1], lop[m, 1])

    def backward(m, modify, consume):
        for parity in range(2):
            for q in range(HALF // CHUNK):
                top = pl.ds(q * CHUNK, CHUNK)
                bot = pl.ds(HALF + q * CHUNK, CHUNK)
                table_rows = pl.ds(parity * HALF + q * CHUNK, CHUNK)
                re, im = modify(table_rows, freq[m, parity, top, :], freq[m, parity, bot, :])
                put_left(m, parity, q * CHUNK, re)
                put_left(m, parity, HALF + q * CHUNK, im)
        tmp[m, 0] = mm(left[2], lop[m, 0])
        tmp[m, 1] = mm(left[3], lop[m, 1])
        for q in range(HALF // CHUNK):
            top = pl.ds(q * CHUNK, CHUNK)
            bot = pl.ds(HALF + q * CHUNK, CHUNK)
            gr, gi = tmp[m, 0, top, :], tmp[m, 0, bot, :]
            hr, hi = tmp[m, 1, top, :], tmp[m, 1, bot, :]
            for rows, re, im in ((top, gr + hr, gi + hi), (bot, gr - hr, gi - hi)):
                put_right(m, 0, rows, jnp.concatenate([re[:, :HALF], im[:, :HALF]], axis=1))
                put_right(m, 1, rows, jnp.concatenate([re[:, HALF:], im[:, HALF:]], axis=1))
        tmp[m, 0] = mm(rop[m, 0], right[0])
        tmp[m, 1] = mm(rop[m, 1], right[1])
        for q in range(FRAME // CHUNK):
            rows = pl.ds(q * CHUNK, CHUNK)
            g, h = tmp[m, 0, rows, :], tmp[m, 1, rows, :]
            re = jnp.concatenate([g[:, :HALF] + h[:, :HALF], g[:, :HALF] - h[:, :HALF]], axis=1)
            im = jnp.concatenate([g[:, HALF:] + h[:, HALF:], g[:, HALF:] - h[:, HALF:]], axis=1)
            consume(m, rows, re, im)

    def times(a_re, a_im, b_re, b_im):
        return a_re * b_re - a_im * b_im, a_re * b_im + a_im * b_re

    def conj_times(a_re, a_im, b_re, b_im):
        return a_re * b_re + a_im * b_im, a_re * b_im - a_im * b_re

    def pair(ref, *at):
        return ref[(*at[:-1], 0, at[-1], slice(None))], ref[(*at[:-1], 1, at[-1], slice(None))]

    def modes(step):
        for m in range(MODES):
            step(m)

    def through_first_slice(f):
        def keep(m, rows, re, im):
            u1[f, m, 0, rows, :] = re
            u1[f, m, 1, rows, :] = im

        modes(lambda m: forward(m, lambda m, rows: times(*pair(probe, m, rows), *pair(obj, f, 0, rows))))
        modes(lambda m: backward(m, lambda rows, re, im: times(kern[0, rows, :], kern[1, rows, :], re, im), keep))

    def keep_wave(f):
        def keep(m, rows, re, im):
            wave[f, m, 0, rows, :] = re
            wave[f, m, 1, rows, :] = im
        return keep

    def terms(f, incoming):
        _, row_shift, _, col_shift = corner(pos_ref, f)
        for q in range(FRAME // CHUNK):
            rows = pl.ds(q * CHUNK, CHUNK)
            total = None
            for m in range(MODES):
                one = conj_times(*incoming(m, rows), *pair(wave, f, m, rows))
                total = one if total is None else (total[0] + one[0], total[1] + one[1])
            for c in range(2):
                padded[c, pl.ds(8 + q * CHUNK, CHUNK), :] = total[c]
        beside = jnp.zeros((TALL, HALF), F32)
        for c in range(2):
            for q in range(264 // TALL):
                x = pltpu.roll(padded[c, pl.ds(q * TALL, TALL + 8), :], lax.rem(TALL + row_shift, TALL + 8), 0)[:TALL]
                x = pltpu.roll(jnp.concatenate([x, beside], axis=1), col_shift, 1)
                for j in range(3):
                    placed[f, c, j, pl.ds(BLANK_ROWS // 8 + q * TALL // 8, TALL // 8)] = x[:, j * HALF:(j + 1) * HALF].reshape(TALL // 8, 8, HALF)

    def collect(s):
        corners = [corner(pos_ref, f) for f in range(2)]

        @pl.loop(0, STRIPS)
        def _(i):
            spots = []
            for block, _, cs, _ in corners:
                j = i - cs
                inside = jnp.logical_and(j >= 0, j < 3)
                spots.append((jnp.where(inside, j, 3), BLANK_ROWS // 8 - block))
            for c in range(2):
                for n in range(ROWS_EXT // 8):
                    x, y = [placed[f, c, j, row + n] for f, (j, row) in enumerate(spots)]
                    gs[s][i, c, pl.ds(n * 8, 8), :] = x + y

    g_out_src, g_sib_src = aligned(384 * me.core), aligned(384 * (1 - me.core))
    g_out_rows, g_sib_rows = aligned(HALO + HALO * me.core), aligned(HALO + HALO * (1 - me.core))

    def strip(half, k):
        return half * 4 + (me.x + k) % 4

    edges, relays, crossing, last = {}, {}, {}, {}

    def start_edges(s, k):
        for h in range(2):
            i = strip(h, k)
            edges[s, k, h, 0] = send.copy(gs[s].at[i, :, pl.ds(g_out_src, HALO), :], edge_out.at[s, k, h], outer)
            edges[s, k, h, 1] = send.copy(gs[s].at[i, :, pl.ds(g_sib_src, HALO), :], edge_sib.at[s, k, h], sibling)

    def take_edges(s, k):
        g = gs[s]
        for h in range(2):
            edges[s, k, h, 0].wait_recv()
            edges[s, k, h, 1].wait_recv()
            i = strip(h, k)
            g[i, :, pl.ds(g_out_rows, HALO), :] += edge_out[s, k, h]
            g[i, :, pl.ds(g_sib_rows, HALO), :] += edge_sib[s, k, h]
        for h in range(2):
            i = strip(h, k)
            if k == 2:
                relays[s, h, 0] = send.copy(g.at[i, 0, mine, :], rb.at[s, h, 0], ahead)
                relays[s, h, 1] = send.copy(g.at[i, 1, mine, :], rb.at[s, h, 1], behind)
            if k == 1:
                crossing[s, h, 0, 1] = send.copy(g.at[i, 1, mine, :], xb.at[s, h, 0, 1], ahead)
            if k == 3:
                crossing[s, h, 1, 0] = send.copy(g.at[i, 0, mine, :], xb.at[s, h, 1, 0], behind)

    def take_relays(s):
        for h in range(2):
            for way, k, peer in ((0, 1, ahead), (1, 3, behind)):
                relays[s, h, way].wait_recv()
                i = strip(h, k)
                gs[s][i, way, mine, :] += rb[s, h, way]
                crossing[s, h, way, way] = send.copy(gs[s].at[i, way, mine, :], xb.at[s, h, way, way], peer)

    def fold(s):
        for h in range(2):
            for way in range(2):
                for c in range(2):
                    crossing[s, h, way, c].wait_recv()
            part[s, h] = gs[s][strip(h, 0), :, mine, :] + xb[s, h, 0] + xb[s, h, 1]
        last[s] = send.copy(part.at[s, 1 - me.zh], zb.at[s], z_peer)

    for s in range(SLICES):
        own_to_z(s)
        own_to_x(s)
    for s in range(SLICES):
        pass_edges(f_own, s, own_ref)
    for load in loads[:4]:
        load.wait()
    perm, perm_t = perms[0], perms[1]
    bg[...] = reorder_exact(back_raw[...], perm, perm_t)
    phase = reorder_exact(phase_raw[...], perm, perm_t)
    kern[0] = jnp.cos(phase)
    kern[1] = jnp.sin(phase)
    from_z(0)
    from_x(own_half, 0)
    from_z(1)
    from_x(own_half, 1)
    for f in range(2):
        half = mm(perm, counts_raw[f].astype(F32).astype(BF16)).astype(BF16)
        cnt[f] = mm(half, perm_t)
    from_x(other_half, 0)
    placed[...] = jnp.zeros_like(placed)
    padded[...] = jnp.zeros_like(padded)
    from_relay(own_half, 0)
    from_relay(other_half, 0)
    for load in loads[4:]:
        load.wait()
    from_relay(own_half, 1)
    cut(0)
    from_x(other_half, 1)
    through_first_slice(0)
    from_relay(other_half, 1)
    through_first_slice(1)
    cut(1)

    @pl.loop(0, 2)
    def _(f):
        modes(lambda m: forward(m, lambda m, rows: times(*pair(u1, f, m, rows), *pair(obj, f, 1, rows))))
        for parity in range(2):
            for q in range(HALF // CHUNK):
                top = pl.ds(q * CHUNK, CHUNK)
                bot = pl.ds(HALF + q * CHUNK, CHUNK)
                rows = pl.ds(parity * HALF + q * CHUNK, CHUNK)
                level = bg[rows, :]
                for m in range(MODES):
                    re, im = freq[m, parity, top, :], freq[m, parity, bot, :]
                    level = level + re * re + im * im
                cnt[f, rows, :] = 1.0 - cnt[f, rows, :] / level
        modes(lambda m: backward(m, lambda rows, re, im: (re * cnt[f, rows, :], im * cnt[f, rows, :]), keep_wave(f)))
        terms(f, lambda m, rows: pair(u1, f, m, rows))

    collect(1)
    for k in (2, 1, 3):
        start_edges(1, k)

    for f in range(2):
        modes(lambda m: forward(m, lambda m, rows: conj_times(*pair(obj, f, 1, rows), *pair(wave, f, m, rows))))
        if f == 0:
            take_edges(1, 2)
        modes(lambda m: backward(m, lambda rows, re, im: conj_times(kern[0, rows, :], kern[1, rows, :], re, im), keep_wave(f)))
        if f == 0:
            take_edges(1, 1)
            take_edges(1, 3)
            start_edges(1, 0)
        terms(f, lambda m, rows: pair(probe, m, rows))
        for m in range(MODES):
            for q in range(FRAME // CHUNK):
                rows = pl.ds(q * CHUNK, CHUNK)
                re, im = conj_times(*pair(obj, f, 0, rows), *pair(wave, f, m, rows))
                if f == 0:
                    p_sum[m, 0, rows, :] = re
                    p_sum[m, 1, rows, :] = im
                else:
                    p_sum[m, 0, rows, :] += re
                    p_sum[m, 1, rows, :] += im
        if f == 0:
            take_relays(1)

    collect(0)
    for k in (2, 1, 3):
        start_edges(0, k)
    other = send.copy(p_sum.at[1 - me.core], sb, sibling)
    take_edges(1, 0)
    start_edges(0, 0)

    quarter = lambda y: pl.ds(aligned(64 * y), 64)
    spot = lambda q: (q // 8, pl.ds(aligned(8 * (q % 8)), 8))
    other.wait_recv()
    ph[...] = p_sum[me.core] + sb[...]
    y_sums = [send.copy(ph.at[:, quarter((me.y + k) % 4), :], yb.at[k - 1], upward[k - 1]) for k in (1, 2, 3)]
    take_edges(0, 2)
    take_edges(0, 1)
    take_edges(0, 3)
    for made in y_sums:
        made.wait_recv()
    pq[...] = ph[:, quarter(me.y), :] + yb[0] + yb[1] + yb[2]
    plane_sums = []
    for j, (q, peer) in enumerate(plane):
        c, rows = spot(q)
        plane_sums.append(send.copy(pq.at[c, rows, :], xzb.at[j], peer))
    fold(1)
    take_relays(0)
    for made in plane_sums:
        made.wait_recv()
    q = me.z * 4 + me.x
    c, rows = spot(q)
    total = pq[c, rows, :]
    for j in range(15):
        total = total + xzb[j]
    final_rows = pl.ds(aligned(64 * me.y + 8 * (q % 8)), 8)
    pout_ref[me.core, c, final_rows, :] = total
    spread = pout_ref.at[me.core, c, final_rows, :]
    plane_gather = [send.copy(spread, spread, peer) for _, peer in plane]
    take_edges(0, 0)
    last[1].wait_recv()
    out_ref[1] = part[1, me.zh] + zb[1]
    for made in plane_gather:
        made.wait_recv()
    spread_y = pout_ref.at[me.core, :, quarter(me.y), :]
    y_gather = [send.copy(spread_y, spread_y, peer) for peer in upward]
    for made in y_gather:
        made.wait_recv()
    final = send.copy(pout_ref.at[me.core], pout_ref.at[me.core], sibling)
    fold(0)
    last[0].wait_recv()
    out_ref[0] = part[0, me.zh] + zb[0]
    final.wait_recv()
    send.finish()


def shards(object_slices, probe_modes, prop_phase, background, positions, counts):
    lefts, rights, perm_pair = dft_constants()
    vmem = pl.BlockSpec(memory_space=pltpu.VMEM)
    square = (FRAME, FRAME)
    half_strip = (2, HALO, HALF)
    full_strip = (2, FRAME, HALF)
    tile = (STRIPS, 2, ROWS_EXT, HALF)
    blocks = (STRIPS, 2, ROWS_EXT // 8, 8, HALF)
    own = object_slices.reshape(SLICES, 2, FRAME // 8, 8, HALF)
    return pl.pallas_call(
        gradient_kernel,
        out_shape=(
            jax.ShapeDtypeStruct((SLICES,) + full_strip, F32),
            jax.ShapeDtypeStruct((MODES, 2) + square, F32),
        ),
        in_specs=[pl.BlockSpec(memory_space=pltpu.SMEM)] + [pl.BlockSpec(memory_space=pl.ANY)] * 8,
        out_specs=(vmem, vmem),
        scratch_shapes=[
            pltpu.VMEM(blocks, F32),
            pltpu.VMEM(blocks, F32),
            pltpu.VMEM(tile, F32),
            pltpu.VMEM(tile, F32),
            pltpu.VMEM((MODES, 2) + square, F32),
            pltpu.VMEM(square, F32),
            pltpu.VMEM(square, F32),
            pltpu.VMEM((2,) + square, jnp.int32),
            pltpu.VMEM((4, FRAME, 3 * FRAME), BF16),
            pltpu.VMEM((4, 3 * FRAME, FRAME), BF16),
            pltpu.VMEM((2,) + square, BF16),
            pltpu.VMEM((2, SLICES, 2) + square, F32),
            pltpu.VMEM((2,) + square, F32),
            pltpu.VMEM(square, F32),
            pltpu.VMEM((2,) + square, F32),
            pltpu.VMEM((2, MODES, 2) + square, F32),
            pltpu.VMEM((2, MODES, 2) + square, F32),
            pltpu.VMEM((MODES, 2, FRAME, 3 * FRAME), BF16),
            pltpu.VMEM((MODES, 2, 3 * FRAME, FRAME), BF16),
            pltpu.VMEM((MODES, 2) + square, F32),
            pltpu.VMEM((MODES, 2) + square, F32),
            pltpu.VMEM((2, FRAME + 16, FRAME), F32),
            pltpu.VMEM((2, 2, 4, PAD_ROWS // 8, 8, HALF), F32),
            pltpu.VMEM((2, 4, 2) + half_strip, F32),
            pltpu.VMEM((2, 4, 2) + half_strip, F32),
            pltpu.VMEM((2, 2, 2, FRAME, HALF), F32),
            pltpu.VMEM((2, 2, 2) + full_strip, F32),
            pltpu.VMEM((2, 2) + full_strip, F32),
            pltpu.VMEM((2,) + full_strip, F32),
            pltpu.VMEM((MODES, 2) + square, F32),
            pltpu.VMEM((2,) + square, F32),
            pltpu.VMEM((2,) + square, F32),
            pltpu.VMEM((3, 2, 64, FRAME), F32),
            pltpu.VMEM((2, 64, FRAME), F32),
            pltpu.VMEM((15, 8, FRAME), F32),
            pltpu.SemaphoreType.DMA((9,)),
            pltpu.SemaphoreType.DMA((COPIES,)),
            pltpu.SemaphoreType.DMA((COPIES,)),
        ],
        compiler_params=pltpu.CompilerParams(collective_id=1, has_side_effects=True, vmem_limit_bytes=60 << 20),
        name="gradient",
    )(positions, own, probe_modes, prop_phase, background, counts,
      jnp.asarray(lefts), jnp.asarray(rights), jnp.asarray(perm_pair))


def solution(mesh):
    in_specs = (
        P(None, None, "tile", "frame"),
        P(),
        P(),
        P(),
        P(("tile", "frame"), None),
        P(("tile", "frame"), None, None),
    )
    out_specs = (P(None, None, "tile", "frame"), P())
    return jax.shard_map(shards, mesh=mesh, in_specs=in_specs, out_specs=out_specs, check_vma=False)
```

time: 436 us -> 136 us (0.31)
  waiting for transfers between devices: 376 us -> 0 us
  Pallas kernels: 24.3 us -> 130 us
  between operations: 13.8 us -> 0.65 us
  local copies, waits for them, and re-layouts: 12.7 us -> 2.93 us
  starting transfers between devices: 5.1 us -> 0 us
    psum x1 -> x0, waiting for transfers between devices: 142 us -> none  [shards(): probe_grad = lax.psum(probe_term, ('tile', 'frame'))]
    reduce_scatter x1 -> x0, waiting for transfers between devices: 113 us -> none  [shards(): summed = lax.psum_scatter(grads, 'frame', scatter_dimension=0, tiled=False)]
    all_gather x1 -> x0, waiting for transfers between devices: 109 us -> none  [shards(): ext = lax.all_gather(strip, 'frame', axis=0, tiled=False)]
    pallas_call x1, Pallas kernels: 24.3 us -> 130 us  [shards(): pl.pallas_call(gradient_kernel, out_shape=(jax.ShapeDtypeStruct((SLICES,)...]
    ppermute x4 -> x0, waiting for transfers between devices: 12.5 us -> none  [shifted(): lax.ppermute(array, axis, [(i, (i + by) % count) for i in range(count)])]
    unnamed x17 -> x4, local copies, waits for them, and re-layouts: 9.49 us -> 2.93 us
    ppermute x4 -> x0, starting transfers between devices: 4.98 us -> none  [shifted(): lax.ppermute(array, axis, [(i, (i + by) % count) for i in range(count)])]
  transfers between devices with their start and end apart: 7 -> 0, of which waited for: 7 -> 0; matrix products, arithmetic and copies ran while one was open for 0% -> 0% of each run, Pallas kernels for 0% -> 0%
where the time goes in v3:
time: 136 us; the launch traced here: 133 us
  Pallas kernels  130 us (96%)
  local copies, waits for them, and re-layouts  2.93 us (2%)
    pallas_call x1, Pallas kernels, shards(): pl.pallas_call(gradient_kernel, out_shape=(jax.ShapeDtypeStruct((SLICES,)...  130 us
    unnamed x4, local copies, waits for them, and re-layouts  2.93 us

profile of v3, /device:TPU:1, one launch (start us, length us, event | category | flops | bytes accessed | tf_op | source)
XLA Modules:
  0.0 133.4 jit_solution(15466006588978110042)
XLA Ops:
  0.6 129.9 %gradient.1 = (f32[2,2,256,128]{3,2,1,0:T(8,128)}, f32[2,2,256,256]{3,2,1,0:T(8,128)}) custom-call(s32[2,2]{1,0:T(2,128)} %pos_ref.1, f32[2,2,32,8,128]{4,3,2,1,0:T(8,128)} %bitcast.1, f32[2,2,256,256]{3,2,1,0:T(8,128)} %probe_in.1, f32[256,256]{1,0:T(8,128)} %phase_in.1, f32[256,256]{1,0:T(8,128)} %back_in.1, s32[2,256,256]{2,1,0:T(8,128)} %counts_in.1, ...), custom_call_target="tpu_custom_call" | custom-call | tf_op jit(solution)/shard_map/gradient/pallas_call | solution.py:560
  130.5 0.0 copy-start
  130.5 2.0 %copy.13 = f32[2,2,256,128]{3,2,1,0:T(8,128)} copy(f32[2,2,256,128]{3,2,1,0:T(8,128)} %get-tuple-element.4) | data formatting | bytes 1048576
  132.5 0.0 copy-done
  132.5 1.0 copy.14
Async XLA Ops:
  130.5 2.0 %copy-start = (f32[2,2,256,256]{3,2,1,0:T(8,128)S(1)}, f32[2,2,256,256]{3,2,1,0:T(8,128)}, u32[]{:S(2)}) copy-start(f32[2,2,256,256]{3,2,1,0:T(8,128)} %get-tuple-element.5) | copy-start | bytes 3145732

commit v4 on v3

--- a/solution.py
+++ b/solution.py
@@ -142,7 +142,7 @@
     return pl.multiple_of(row, 8)
 
 
-GATHER_COPIES = 6 + 4 + 8 + 32
+GATHER_COPIES = 6 + 4 + 8 + 16 + 4
 SCATTER_COPIES = 32 + 8 + 16 + 2 + 1 + 3 + 15 + 15 + 3 + 1
 COPIES = GATHER_COPIES + SCATTER_COPIES
 
@@ -190,10 +190,15 @@
     def pass_edges(strip, s, ref=None):
         base = exts[s].at[strip] if ref is None else ref.at[s]
         shift = 0 if ref is None else 16
-        for src, dst, peer in ((out_src, out_dst, outer), (sib_src, sib_dst, sibling)):
-            margins[s].append(send.copy(
-                base.at[:, pl.ds(src - shift, 16)], exts[s].at[strip, :, pl.ds(dst, 16)], peer
-            ))
+        margins[s].append(send.copy(
+            base.at[:, pl.ds(out_src - shift, 16)], exts[s].at[strip, :, pl.ds(out_dst, 16)], outer
+        ))
+
+    def pass_half(which, s):
+        group = exts[s].at[pl.ds(half_of[which] * 4, 4)]
+        margins[s].append(send.copy(
+            group.at[:, :, pl.ds(sib_src, 16)], group.at[:, :, pl.ds(sib_dst, 16)], sibling
+        ))
 
     to_z, to_x, relayed = {}, {}, {}
     own_half, other_half = 0, 1
@@ -225,12 +230,14 @@
             pass_edges(strip_at(which, k), s)
 
     def from_relay(which, s):
+        if which == own_half:
+            keeps[s].wait()
         for way in range(2):
             relayed[which, s, way].wait_recv()
         pass_edges(strip_at(which, 2), s)
+        pass_half(which, s)
 
     def cut(s):
-        keeps[s].wait()
         for made in margins[s]:
             made.wait_recv()
 
@@ -378,6 +385,7 @@
         return half * 4 + (me.x + k) % 4
 
     edges, relays, crossing, last = {}, {}, {}, {}
+    half_order = (1 - me.zh, me.zh)
 
     def start_edges(s, k):
         for h in range(2):
@@ -393,61 +401,69 @@
             i = strip(h, k)
             g[i, :, pl.ds(g_out_rows, HALO), :] += edge_out[s, k, h]
             g[i, :, pl.ds(g_sib_rows, HALO), :] += edge_sib[s, k, h]
-        for h in range(2):
+        for n, h in enumerate(half_order):
             i = strip(h, k)
             if k == 2:
-                relays[s, h, 0] = send.copy(g.at[i, 0, mine, :], rb.at[s, h, 0], ahead)
-                relays[s, h, 1] = send.copy(g.at[i, 1, mine, :], rb.at[s, h, 1], behind)
+                relays[s, n, 0] = send.copy(g.at[i, 0, mine, :], rb.at[s, n, 0], ahead)
+                relays[s, n, 1] = send.copy(g.at[i, 1, mine, :], rb.at[s, n, 1], behind)
             if k == 1:
-                crossing[s, h, 0, 1] = send.copy(g.at[i, 1, mine, :], xb.at[s, h, 0, 1], ahead)
+                crossing[s, n, 0, 1] = send.copy(g.at[i, 1, mine, :], xb.at[s, n, 0, 1], ahead)
             if k == 3:
-                crossing[s, h, 1, 0] = send.copy(g.at[i, 0, mine, :], xb.at[s, h, 1, 0], behind)
+                crossing[s, n, 1, 0] = send.copy(g.at[i, 0, mine, :], xb.at[s, n, 1, 0], behind)
 
     def take_relays(s):
-        for h in range(2):
+        for n, h in enumerate(half_order):
             for way, k, peer in ((0, 1, ahead), (1, 3, behind)):
-                relays[s, h, way].wait_recv()
+                relays[s, n, way].wait_recv()
                 i = strip(h, k)
-                gs[s][i, way, mine, :] += rb[s, h, way]
-                crossing[s, h, way, way] = send.copy(gs[s].at[i, way, mine, :], xb.at[s, h, way, way], peer)
+                gs[s][i, way, mine, :] += rb[s, n, way]
+                crossing[s, n, way, way] = send.copy(gs[s].at[i, way, mine, :], xb.at[s, n, way, way], peer)
+
+    def take_crossing(s, n):
+        for way in range(2):
+            for c in range(2):
+                crossing[s, n, way, c].wait_recv()
+        return gs[s][strip(half_order[n], 0), :, mine, :] + xb[s, n, 0] + xb[s, n, 1]
 
     def fold(s):
-        for h in range(2):
-            for way in range(2):
-                for c in range(2):
-                    crossing[s, h, way, c].wait_recv()
-            part[s, h] = gs[s][strip(h, 0), :, mine, :] + xb[s, h, 0] + xb[s, h, 1]
-        last[s] = send.copy(part.at[s, 1 - me.zh], zb.at[s], z_peer)
-
-    for s in range(SLICES):
-        own_to_z(s)
-        own_to_x(s)
-    for s in range(SLICES):
-        pass_edges(f_own, s, own_ref)
+        part[s] = take_crossing(s, 0)
+        last[s] = send.copy(part.at[s], zb.at[s], z_peer)
+
+    def finish(s):
+        own_sum = take_crossing(s, 1)
+        last[s].wait_recv()
+        out_ref[s] = own_sum + zb[s]
+
+    own_to_z(0)
+    own_to_x(0)
+    own_to_z(1)
+    own_to_x(1)
+    pass_edges(f_own, 0, own_ref)
     for load in loads[:4]:
         load.wait()
     perm, perm_t = perms[0], perms[1]
     bg[...] = reorder_exact(back_raw[...], perm, perm_t)
     phase = reorder_exact(phase_raw[...], perm, perm_t)
+    from_z(0)
+    from_x(own_half, 0)
     kern[0] = jnp.cos(phase)
     kern[1] = jnp.sin(phase)
-    from_z(0)
-    from_x(own_half, 0)
     from_z(1)
-    from_x(own_half, 1)
     for f in range(2):
         half = mm(perm, counts_raw[f].astype(F32).astype(BF16)).astype(BF16)
         cnt[f] = mm(half, perm_t)
+    from_x(own_half, 1)
+    padded[...] = jnp.zeros_like(padded)
+    placed[...] = jnp.zeros_like(placed)
     from_x(other_half, 0)
-    placed[...] = jnp.zeros_like(placed)
-    padded[...] = jnp.zeros_like(padded)
     from_relay(own_half, 0)
     from_relay(other_half, 0)
+    pass_edges(f_own, 1, own_ref)
     for load in loads[4:]:
         load.wait()
+    from_x(other_half, 1)
     from_relay(own_half, 1)
     cut(0)
-    from_x(other_half, 1)
     through_first_slice(0)
     from_relay(other_half, 1)
     through_first_slice(1)
@@ -470,18 +486,19 @@
         terms(f, lambda m, rows: pair(u1, f, m, rows))
 
     collect(1)
-    for k in (2, 1, 3):
+    for k in (2, 1, 3, 0):
         start_edges(1, k)
 
     for f in range(2):
         modes(lambda m: forward(m, lambda m, rows: conj_times(*pair(obj, f, 1, rows), *pair(wave, f, m, rows))))
         if f == 0:
             take_edges(1, 2)
+        else:
+            take_relays(1)
         modes(lambda m: backward(m, lambda rows, re, im: conj_times(kern[0, rows, :], kern[1, rows, :], re, im), keep_wave(f)))
         if f == 0:
             take_edges(1, 1)
             take_edges(1, 3)
-            start_edges(1, 0)
         terms(f, lambda m, rows: pair(probe, m, rows))
         for m in range(MODES):
             for q in range(FRAME // CHUNK):
@@ -493,22 +510,19 @@
                 else:
                     p_sum[m, 0, rows, :] += re
                     p_sum[m, 1, rows, :] += im
-        if f == 0:
-            take_relays(1)
-
+
+    other = send.copy(p_sum.at[1 - me.core], sb, sibling)
     collect(0)
     for k in (2, 1, 3):
         start_edges(0, k)
-    other = send.copy(p_sum.at[1 - me.core], sb, sibling)
-    take_edges(1, 0)
-    start_edges(0, 0)
-
     quarter = lambda y: pl.ds(aligned(64 * y), 64)
     spot = lambda q: (q // 8, pl.ds(aligned(8 * (q % 8)), 8))
     other.wait_recv()
     ph[...] = p_sum[me.core] + sb[...]
     y_sums = [send.copy(ph.at[:, quarter((me.y + k) % 4), :], yb.at[k - 1], upward[k - 1]) for k in (1, 2, 3)]
+    start_edges(0, 0)
     take_edges(0, 2)
+    take_edges(1, 0)
     take_edges(0, 1)
     take_edges(0, 3)
     for made in y_sums:
@@ -518,8 +532,9 @@
     for j, (q, peer) in enumerate(plane):
         c, rows = spot(q)
         plane_sums.append(send.copy(pq.at[c, rows, :], xzb.at[j], peer))
+    take_relays(0)
     fold(1)
-    take_relays(0)
+    take_edges(0, 0)
     for made in plane_sums:
         made.wait_recv()
     q = me.z * 4 + me.x
@@ -531,19 +546,16 @@
     pout_ref[me.core, c, final_rows, :] = total
     spread = pout_ref.at[me.core, c, final_rows, :]
     plane_gather = [send.copy(spread, spread, peer) for _, peer in plane]
-    take_edges(0, 0)
-    last[1].wait_recv()
-    out_ref[1] = part[1, me.zh] + zb[1]
+    finish(1)
     for made in plane_gather:
         made.wait_recv()
     spread_y = pout_ref.at[me.core, :, quarter(me.y), :]
     y_gather = [send.copy(spread_y, spread_y, peer) for peer in upward]
+    fold(0)
     for made in y_gather:
         made.wait_recv()
     final = send.copy(pout_ref.at[me.core], pout_ref.at[me.core], sibling)
-    fold(0)
-    last[0].wait_recv()
-    out_ref[0] = part[0, me.zh] + zb[0]
+    finish(0)
     final.wait_recv()
     send.finish()
 
@@ -593,7 +605,7 @@
             pltpu.VMEM((2, 4, 2) + half_strip, F32),
             pltpu.VMEM((2, 2, 2, FRAME, HALF), F32),
             pltpu.VMEM((2, 2, 2) + full_strip, F32),
-            pltpu.VMEM((2, 2) + full_strip, F32),
+            pltpu.VMEM((2,) + full_strip, F32),
             pltpu.VMEM((2,) + full_strip, F32),
             pltpu.VMEM((MODES, 2) + square, F32),
             pltpu.VMEM((2,) + square, F32),

time: 136 us -> 128 us (0.941); the launches traced: 133 us -> 128 us
  Pallas kernels: 130 us -> 124 us
    pallas_call x1, Pallas kernels: 130 us -> 124 us  [shards(): pl.pallas_call(gradient_kernel, out_shape=(jax.ShapeDtypeStruct((SLICES,)...]
where the time goes in v4:
time: 128 us
  Pallas kernels  124 us (97%)
  local copies, waits for them, and re-layouts  2.93 us (2%)
    pallas_call x1, Pallas kernels, shards(): pl.pallas_call(gradient_kernel, out_shape=(jax.ShapeDtypeStruct((SLICES,)...  124 us
    unnamed x4, local copies, waits for them, and re-layouts  2.93 us

profile of v4, /device:TPU:1, one launch (start us, length us, event | category | flops | bytes accessed | tf_op | source)
XLA Modules:
  0.0 127.5 jit_solution(11879463637039534357)
XLA Ops:
  0.6 123.9 %gradient.1 = (f32[2,2,256,128]{3,2,1,0:T(8,128)}, f32[2,2,256,256]{3,2,1,0:T(8,128)}) custom-call(s32[2,2]{1,0:T(2,128)} %pos_ref.1, f32[2,2,32,8,128]{4,3,2,1,0:T(8,128)} %bitcast.1, f32[2,2,256,256]{3,2,1,0:T(8,128)} %probe_in.1, f32[256,256]{1,0:T(8,128)} %phase_in.1, f32[256,256]{1,0:T(8,128)} %back_in.1, s32[2,256,256]{2,1,0:T(8,128)} %counts_in.1, ...), custom_call_target="tpu_custom_call" | custom-call | tf_op jit(solution)/shard_map/gradient/pallas_call | solution.py:572
  124.6 0.0 copy-start
  124.6 2.0 %copy.13 = f32[2,2,256,128]{3,2,1,0:T(8,128)} copy(f32[2,2,256,128]{3,2,1,0:T(8,128)} %get-tuple-element.4) | data formatting | bytes 1048576
  126.5 0.0 copy-done
  126.5 1.0 copy.14
Async XLA Ops:
  124.6 2.0 %copy-start = (f32[2,2,256,256]{3,2,1,0:T(8,128)S(1)}, f32[2,2,256,256]{3,2,1,0:T(8,128)}, u32[]{:S(2)}) copy-start(f32[2,2,256,256]{3,2,1,0:T(8,128)} %get-tuple-element.5) | copy-start | bytes 3145732

commit v5 on v4

--- a/solution.py
+++ b/solution.py
@@ -279,6 +279,7 @@
             put_right(m, 1, rows, jnp.concatenate([a - b, c - d], axis=1))
         tmp[m, 0] = mm(rop[m, 0], right[2])
         tmp[m, 1] = mm(rop[m, 1], right[3])
+        yield
         for q in range(HALF // CHUNK):
             top = pl.ds(q * CHUNK, CHUNK)
             bot = pl.ds(HALF + q * CHUNK, CHUNK)
@@ -289,6 +290,7 @@
                 put_left(m, parity, HALF + q * CHUNK, jnp.concatenate([e[:, HALF:], o[:, HALF:]], axis=1))
         freq[m, 0] = mm(left[0], lop[m, 0])
         freq[m, 1] = mm(left[1], lop[m, 1])
+        yield
 
     def backward(m, modify, consume):
         for parity in range(2):
@@ -301,6 +303,7 @@
                 put_left(m, parity, HALF + q * CHUNK, im)
         tmp[m, 0] = mm(left[2], lop[m, 0])
         tmp[m, 1] = mm(left[3], lop[m, 1])
+        yield
         for q in range(HALF // CHUNK):
             top = pl.ds(q * CHUNK, CHUNK)
             bot = pl.ds(HALF + q * CHUNK, CHUNK)
@@ -311,6 +314,7 @@
                 put_right(m, 1, rows, jnp.concatenate([re[:, HALF:], im[:, HALF:]], axis=1))
         tmp[m, 0] = mm(rop[m, 0], right[0])
         tmp[m, 1] = mm(rop[m, 1], right[1])
+        yield
         for q in range(FRAME // CHUNK):
             rows = pl.ds(q * CHUNK, CHUNK)
             g, h = tmp[m, 0, rows, :], tmp[m, 1, rows, :]
@@ -327,17 +331,21 @@
     def pair(ref, *at):
         return ref[(*at[:-1], 0, at[-1], slice(None))], ref[(*at[:-1], 1, at[-1], slice(None))]
 
-    def modes(step):
-        for m in range(MODES):
-            step(m)
+    def modes(*steps):
+        def chain(m):
+            for step in steps:
+                yield from step(m)
+
+        running = [chain(m) for m in range(MODES)]
+        while running:
+            running = [one for one in running if next(one, True) is None]
 
     def through_first_slice(f):
         def keep(m, rows, re, im):
             u1[f, m, 0, rows, :] = re
             u1[f, m, 1, rows, :] = im
 
-        modes(lambda m: forward(m, lambda m, rows: times(*pair(probe, m, rows), *pair(obj, f, 0, rows))))
-        modes(lambda m: backward(m, lambda rows, re, im: times(kern[0, rows, :], kern[1, rows, :], re, im), keep))
+        modes(lambda m: forward(m, lambda m, rows: times(*pair(probe, m, rows), *pair(obj, f, 0, rows))), lambda m: backward(m, lambda rows, re, im: times(kern[0, rows, :], kern[1, rows, :], re, im), keep))
 
     def keep_wave(f):
         def keep(m, rows, re, im):
@@ -464,8 +472,8 @@
     from_x(other_half, 1)
     from_relay(own_half, 1)
     cut(0)
+    from_relay(other_half, 1)
     through_first_slice(0)
-    from_relay(other_half, 1)
     through_first_slice(1)
     cut(1)
 

time: 128 us -> 126 us (0.984)
  Pallas kernels: 124 us -> 122 us
    pallas_call x1, Pallas kernels: 124 us -> 122 us  [shards(): pl.pallas_call(gradient_kernel, out_shape=(jax.ShapeDtypeStruct((SLICES,)...]
where the time goes in v5:
time: 126 us
  Pallas kernels  122 us (97%)
  local copies, waits for them, and re-layouts  2.93 us (2%)
    pallas_call x1, Pallas kernels, shards(): pl.pallas_call(gradient_kernel, out_shape=(jax.ShapeDtypeStruct((SLICES,)...  122 us
    unnamed x4, local copies, waits for them, and re-layouts  2.93 us

profile of v5, /device:TPU:1, one launch (start us, length us, event | category | flops | bytes accessed | tf_op | source)
XLA Modules:
  0.0 125.6 jit_solution(6806355491274829450)
XLA Ops:
  0.6 122.0 %gradient.1 = (f32[2,2,256,128]{3,2,1,0:T(8,128)}, f32[2,2,256,256]{3,2,1,0:T(8,128)}) custom-call(s32[2,2]{1,0:T(2,128)} %pos_ref.1, f32[2,2,32,8,128]{4,3,2,1,0:T(8,128)} %bitcast.1, f32[2,2,256,256]{3,2,1,0:T(8,128)} %probe_in.1, f32[256,256]{1,0:T(8,128)} %phase_in.1, f32[256,256]{1,0:T(8,128)} %back_in.1, s32[2,256,256]{2,1,0:T(8,128)} %counts_in.1, ...), custom_call_target="tpu_custom_call" | custom-call | tf_op jit(solution)/shard_map/gradient/pallas_call | solution.py:580
  122.7 0.0 copy-start
  122.7 2.0 %copy.13 = f32[2,2,256,128]{3,2,1,0:T(8,128)} copy(f32[2,2,256,128]{3,2,1,0:T(8,128)} %get-tuple-element.4) | data formatting | bytes 1048576
  124.6 0.0 copy-done
  124.6 1.0 copy.14
Async XLA Ops:
  122.7 2.0 %copy-start = (f32[2,2,256,256]{3,2,1,0:T(8,128)S(1)}, f32[2,2,256,256]{3,2,1,0:T(8,128)}, u32[]{:S(2)}) copy-start(f32[2,2,256,256]{3,2,1,0:T(8,128)} %get-tuple-element.5) | copy-start | bytes 3145732

commit v6 on v5

--- a/solution.py
+++ b/solution.py
@@ -149,10 +149,10 @@
 
 def gradient_kernel(
     pos_ref, own_ref, probe_in, phase_in, back_in, counts_in, left_in, right_in, perm_in,
-    out_ref, pout_ref,
+    out_ref, zb, pout_ref,
     ext_0, ext_1, g_0, g_1, probe, phase_raw, back_raw, counts_raw, left, right, perms,
     obj, kern, bg, cnt, wave, u1, rop, lop, tmp, freq, padded, placed,
-    edge_out, edge_sib, rb, xb, part, zb, p_sum, sb, ph, yb, pq, xzb,
+    edge_out, edge_sib, rb, xb, part, p_sum, sb, ph, yb, pq, xzb,
     local_sems, send_sems, recv_sems,
 ):
     exts, gs = (ext_0, ext_1), (g_0, g_1)
@@ -438,9 +438,8 @@
         last[s] = send.copy(part.at[s], zb.at[s], z_peer)
 
     def finish(s):
-        own_sum = take_crossing(s, 1)
+        out_ref[s] = take_crossing(s, 1)
         last[s].wait_recv()
-        out_ref[s] = own_sum + zb[s]
 
     own_to_z(0)
     own_to_x(0)
@@ -577,14 +576,15 @@
     tile = (STRIPS, 2, ROWS_EXT, HALF)
     blocks = (STRIPS, 2, ROWS_EXT // 8, 8, HALF)
     own = object_slices.reshape(SLICES, 2, FRAME // 8, 8, HALF)
-    return pl.pallas_call(
+    near, far, probe_grad = pl.pallas_call(
         gradient_kernel,
         out_shape=(
+            jax.ShapeDtypeStruct((SLICES,) + full_strip, F32),
             jax.ShapeDtypeStruct((SLICES,) + full_strip, F32),
             jax.ShapeDtypeStruct((MODES, 2) + square, F32),
         ),
         in_specs=[pl.BlockSpec(memory_space=pltpu.SMEM)] + [pl.BlockSpec(memory_space=pl.ANY)] * 8,
-        out_specs=(vmem, vmem),
+        out_specs=(vmem, vmem, vmem),
         scratch_shapes=[
             pltpu.VMEM(blocks, F32),
             pltpu.VMEM(blocks, F32),
@@ -614,7 +614,6 @@
             pltpu.VMEM((2, 2, 2, FRAME, HALF), F32),
             pltpu.VMEM((2, 2, 2) + full_strip, F32),
             pltpu.VMEM((2,) + full_strip, F32),
-            pltpu.VMEM((2,) + full_strip, F32),
             pltpu.VMEM((MODES, 2) + square, F32),
             pltpu.VMEM((2,) + square, F32),
             pltpu.VMEM((2,) + square, F32),
@@ -629,6 +628,7 @@
         name="gradient",
     )(positions, own, probe_modes, prop_phase, background, counts,
       jnp.asarray(lefts), jnp.asarray(rights), jnp.asarray(perm_pair))
+    return near + far, probe_grad
 
 
 def solution(mesh):

time: 126 us -> 126 us (level)
  other arithmetic: 0 us -> 2.13 us
  local copies, waits for them, and re-layouts: 2.93 us -> 0.97 us
    add x0 -> x1, other arithmetic: none -> 2.13 us  [shards(): return (near + far, probe_grad)]
    unnamed x4 -> x3, local copies, waits for them, and re-layouts: 2.93 us -> 0.97 us
where the time goes in v6:
time: 126 us
  Pallas kernels  122 us (97%)
  other arithmetic  2.13 us (2%)
    pallas_call x1, Pallas kernels, shards(): pl.pallas_call(gradient_kernel, out_shape=(jax.ShapeDtypeStruct((SLICES,)...  122 us

profile of v6, /device:TPU:1, one launch (start us, length us, event | category | flops | bytes accessed | tf_op | source)
XLA Modules:
  0.0 125.9 jit_solution(17331688336655257077)
XLA Ops:
  0.6 122.2 %gradient.1 = (f32[2,2,256,128]{3,2,1,0:T(8,128)}, f32[2,2,256,128]{3,2,1,0:T(8,128)}, f32[2,2,256,256]{3,2,1,0:T(8,128)}) custom-call(s32[2,2]{1,0:T(2,128)} %pos_ref.1, f32[2,2,32,8,128]{4,3,2,1,0:T(8,128)} %bitcast.1, f32[2,2,256,256]{3,2,1,0:T(8,128)} %probe_in.1, f32[256,256]{1,0:T(8,128)} %phase_in.1, f32[256,256]{1,0:T(8,128)} %back_in.1, ...), custom_call_target="tpu_custom_call" | custom-call | tf_op jit(solution)/shard_map/gradient/pallas_call | solution.py:579
  122.8 0.0 copy-start
  122.8 2.1 %add.3 = f32[2,2,256,128]{3,2,1,0:T(8,128)} add(f32[2,2,256,128]{3,2,1,0:T(8,128)} %get-tuple-element.5, f32[2,2,256,128]{3,2,1,0:T(8,128)} %get-tuple-element.6) | non-fusion elementwise | flops 131072 | bytes 1572864 | tf_op jit(solution)/shard_map/add | solution.py:631
  125.0 0.0 copy-done
  125.0 1.0 copy.12
Async XLA Ops:
  122.8 2.1 %copy-start = (f32[2,2,256,256]{3,2,1,0:T(8,128)S(1)}, f32[2,2,256,256]{3,2,1,0:T(8,128)}, u32[]{:S(2)}) copy-start(f32[2,2,256,256]{3,2,1,0:T(8,128)} %get-tuple-element.11) | copy-start | bytes 3145732
